TPU v7x, 256 devices: a whole 4x4x8 slice. The times are simulated.
256 devices in a mesh: dp: 2 (over y_lo), seq: 128 (over x, y_hi, z, core).
Axes of the slice: x: 4, y: 4 (y_hi: 2, y_lo: 2; y = y_hi * 2 + y_lo), z: 8, core: 2. Of those that a mesh axis runs over, the one named last changes fastest.
Arguments:
- tokens: bfloat16 [2, 128, 512, 384], P('dp', 'seq'), may hold values from -6 to 6
- cotangent: bfloat16 [2, 128, 512, 384], P('dp', 'seq'), may hold values from -6 to 6
- wqkv_spatial: bfloat16 [384, 1152], replicated, may hold values from -12.5 to 12.5
- wo_spatial: bfloat16 [384, 384], replicated, may hold values from -0.3125 to 0.3125
- wqkv_temporal: bfloat16 [384, 1152], replicated, may hold values from -12.5 to 12.5
- wo_temporal: bfloat16 [384, 384], replicated, may hold values from -0.3125 to 0.3125
Outputs:
- token_grad: bfloat16 [2, 128, 512, 384], P('dp', 'seq')
- grad_wqkv_spatial: float32 [384, 1152], P(None, 'seq')
- grad_wo_spatial: float32 [384, 384], P(None, 'seq')
- grad_wqkv_temporal: float32 [384, 1152], P(None, 'seq')
- grad_wo_temporal: float32 [384, 384], P(None, 'seq')
All inputs are finite; a program needn't handle non-finite values.
Results may differ from a plain program's by a relative error of at most 0.015.
Values may be sent and summed in bfloat16 or wider, within the bound.
No kernel may reach another device: no remote copies, remote signals or barrier semaphores. Data moves between devices by JAX's collectives and lax.ppermute only.
A program may use at most 64 MiB of HBM per device.

v0:
```python
import functools

import jax
import jax.numpy as jnp
import numpy as np
from jax import lax
from jax.experimental import pallas as pl
from jax.experimental.pallas import tpu as pltpu
from jax.sharding import PartitionSpec as P

HEADS = 6
F32 = jnp.float32
B16 = jnp.bfloat16
NN = (((1,), (0,)), ((), ()))
NT = (((1,), (1,)), ((), ()))
VM = pl.BlockSpec(memory_space=pltpu.VMEM)


def mm(left, right, dims=NN):
    return lax.dot_general(left, right, dims, preferred_element_type=F32)


def normalize(values):
    average = jnp.mean(values, -1, keepdims=True)
    centered = values - average
    spread = jnp.mean(centered * centered, -1, keepdims=True)
    inverse = lax.rsqrt(spread + 1e-06)
    return centered * inverse, inverse


def normalize_back(scaled, inverse, upstream):
    return inverse * (
        upstream
        - jnp.mean(upstream, -1, keepdims=True)
        - scaled * jnp.mean(upstream * scaled, -1, keepdims=True)
    )


def one_head(block, sub, half, rows_axis):
    at = lax.broadcasted_iota(jnp.int32, block.shape, rows_axis)
    keep = (at < half) if sub == 0 else (at >= half)
    return jnp.where(keep, block, jnp.zeros_like(block))


def softmax_rows(scores):
    e = jnp.exp(scores - jnp.max(scores, 0, keepdims=True))
    return (e * (1.0 / jnp.sum(e, 0, keepdims=True))).astype(B16)


def score_back(probs, prob_grad):
    weights = probs.astype(F32)
    total = jnp.sum(weights * prob_grad, 0, keepdims=True)
    return (weights * (prob_grad - total)).astype(B16)


def both_heads(block, half, rows_axis, join_axis):
    return jnp.concatenate(
        [one_head(block, 0, half, rows_axis), one_head(block, 1, half, rows_axis)], join_axis
    )


def regroup(count, inner, outer):
    row = lax.broadcasted_iota(jnp.int32, (count, count), 0)
    column = lax.broadcasted_iota(jnp.int32, (count, count), 1)
    source = (row & (inner - 1)) * outer + lax.shift_right_logical(row, inner.bit_length() - 1)
    return (column == source).astype(F32).astype(B16)


HBM = pl.BlockSpec(memory_space=pltpu.HBM)


def call(kernel, arrays, outs, in_specs, out_specs, scratch, copies, flops, exps=0):
    return pl.pallas_call(
        kernel,
        out_shape=tuple(jax.ShapeDtypeStruct(shape, B16) for shape in outs),
        in_specs=in_specs,
        out_specs=tuple(out_specs),
        scratch_shapes=[pltpu.VMEM(shape, B16) for shape in scratch]
        + [pltpu.SemaphoreType.DMA((copies,))],
        cost_estimate=pl.CostEstimate(
            flops=flops,
            bytes_accessed=sum(array.size * 2 for array in arrays),
            transcendentals=exps,
        ),
    )(*arrays)


class Copies:
    def __init__(self, sems):
        self.sems, self.pending = sems, []

    def start(self, source, target):
        copy = pltpu.make_async_copy(source, target, self.sems.at[len(self.pending)])
        self.pending.append(copy)
        copy.start()
        return copy


def spatial_forward_kernel(
    tok_hbm, cot_hbm, w_hbm, wo_hbm, slab_ref, comb_hbm, att_hbm, probs_hbm,
    tok_ref, cot_ref, w_ref, wo_ref, comb_ref, att_ref, probs_ref, sems,
):
    copies = Copies(sems)
    tok_in = copies.start(tok_hbm, tok_ref)
    w_in = copies.start(w_hbm, w_ref)
    wo_in = copies.start(wo_hbm, wo_ref)
    cot_in = copies.start(cot_hbm, cot_ref)
    width = tok_ref.shape[-1]
    hw = width // HEADS
    outs = []
    tok_in.wait()
    x = tok_ref[...].astype(F32)
    scaled, _ = normalize(x)
    w_in.wait()
    comb = mm(scaled.astype(B16), w_ref[...]).astype(B16)
    comb_ref[...] = comb
    outs.append(copies.start(comb_ref, comb_hbm))
    qt = (comb[:, :width] * (hw ** -0.5)).T
    vt = comb[:, 2 * width :].T
    parts = []
    for pair in range(HEADS // 2):
        at = pair * 2 * hw
        keys = comb[:, width + at : width + at + 2 * hw]
        for sub in range(2):
            head = 2 * pair + sub
            p = softmax_rows(mm(keys, one_head(qt[at : at + 2 * hw], sub, hw, 0)))
            probs_ref[head] = p
            outs.append(copies.start(probs_ref.at[head], probs_hbm.at[head]))
            parts.append(mm(vt[head * hw : (head + 1) * hw], p).astype(B16))
    att = jnp.concatenate(parts, 0).T
    att_ref[...] = att
    outs.append(copies.start(att_ref, att_hbm))
    wo_in.wait()
    out = (x + mm(att, wo_ref[...])).astype(B16)
    cot_in.wait()
    half = (slab_ref.shape[0], slab_ref.shape[1] // 2, width)
    slab_ref[...] = jnp.concatenate([out.reshape(half), cot_ref[...].reshape(half)], 1)
    for copy in outs:
        copy.wait()


def spatial_forward(tokens, cotangent, w, wo, slab):
    rows, width = tokens.shape
    wide, square = (rows, 3 * width), (rows, width)
    probs = (HEADS, rows, rows)
    return call(
        spatial_forward_kernel, (tokens, cotangent, w, wo),
        (slab, wide, square, probs), [HBM] * 4, [VM] + [HBM] * 3,
        [square, square, w.shape, wo.shape, wide, square, probs],
        6 + HEADS, 2_000_000_000, 1_600_000,
    )


def temporal_kernel(
    slab_ref, w_hbm, wo_hbm, branch_ref, normed_hbm, cot_hbm, att_hbm, dct_hbm,
    w_ref, wo_ref, normed_ref, cot_ref, att_ref, dct_ref, sems,
):
    copies = Copies(sems)
    w_in = copies.start(w_hbm, w_ref)
    wo_in = copies.start(wo_hbm, wo_ref)
    frames, both, width = slab_ref.shape
    patches = both // 2
    rows = frames * patches
    hw = width // HEADS
    gather = regroup(rows, frames, patches)
    slab = slab_ref[...]
    x = mm(gather, slab[:, :patches].reshape(rows, width))
    cot = mm(gather, slab[:, patches:].reshape(rows, width)).astype(B16)
    cot_ref[...] = cot
    outs = [copies.start(cot_ref, cot_hbm)]
    scaled, inverse = normalize(x)
    normed = scaled.astype(B16)
    normed_ref[...] = normed
    outs.append(copies.start(normed_ref, normed_hbm))
    w_in.wait()
    comb = mm(normed, w_ref[...]).astype(B16)
    wo_in.wait()
    g = mm(cot, wo_ref[...], NT).astype(B16)
    q = comb[:, :width] * (hw ** -0.5)
    k = comb[:, width : 2 * width]
    v = comb[:, 2 * width :]
    qt, kt, vt, gt = q.T, k.T, v.T, g.T
    dqt_parts, att_parts, dk_parts, dv_parts = [], [], [], []
    for patch in range(patches):
        here = slice(patch * frames, (patch + 1) * frames)
        dqt_p, att_p, dk_p, dv_p = [], [], [], []
        for pair in range(HEADS // 2):
            lanes = slice(pair * 2 * hw, (pair + 1) * 2 * hw)
            p = softmax_rows(mm(k[here, lanes], both_heads(qt[lanes, here], hw, 0, 1)))
            dp = mm(v[here, lanes], both_heads(gt[lanes, here], hw, 0, 1))
            ds = score_back(p, dp)
            for sub in range(2):
                own = slice((2 * pair + sub) * hw, (2 * pair + sub + 1) * hw)
                cols = slice(sub * frames, (sub + 1) * frames)
                att_p.append(mm(vt[own, here], p[:, cols]).astype(B16))
                dqt_p.append((mm(kt[own, here], ds[:, cols]) * (hw ** -0.5)).astype(B16))
            dk_p.append(mm(ds, both_heads(q[here, lanes], hw, 1, 0)).astype(B16))
            dv_p.append(mm(p, both_heads(g[here, lanes], hw, 1, 0)).astype(B16))
        dqt_parts.append(jnp.concatenate(dqt_p, 0))
        att_parts.append(jnp.concatenate(att_p, 0))
        dk_parts.append(jnp.concatenate(dk_p, 1))
        dv_parts.append(jnp.concatenate(dv_p, 1))
    dqt = jnp.concatenate(dqt_parts, 1)
    att_ref[...] = jnp.concatenate(att_parts, 1).T
    outs.append(copies.start(att_ref, att_hbm))
    dk = jnp.concatenate(dk_parts, 0)
    dv = jnp.concatenate(dv_parts, 0)
    dct_ref[:width] = dqt
    dct_ref[width : 2 * width] = dk.T
    dct_ref[2 * width :] = dv.T
    outs.append(copies.start(dct_ref, dct_hbm))
    u = (
        mm(dqt.T, w_ref[:, :width], NT)
        + mm(dk, w_ref[:, width : 2 * width], NT)
        + mm(dv, w_ref[:, 2 * width :], NT)
    )
    branch = normalize_back(scaled, inverse, u).astype(B16)
    scatter = regroup(rows, patches, frames)
    branch_ref[...] = mm(scatter, branch).astype(B16).reshape(branch_ref.shape)
    for copy in outs:
        copy.wait()


def temporal(slab, w, wo):
    frames, both, width = slab.shape
    rows = frames * both // 2
    square = (rows, width)
    return call(
        temporal_kernel, (slab, w, wo),
        ((frames, both // 2, width), square, square, square, (3 * width, rows)),
        [VM, HBM, HBM], [VM] + [HBM] * 4,
        [w.shape, wo.shape, square, square, square, (3 * width, rows)],
        6, 3_000_000_000, 400_000,
    )


def spread(copies, onehot, gq, go, slab_ref, own_hbm, send_hbm):
    here = lax.axis_index("seq") % slab_ref.shape[0]
    groups = slab_ref.shape[1]
    a, b = gq.shape[0] // groups, go.shape[0] // groups
    outs = []
    for x in range(groups):
        source = jnp.concatenate([gq[x * a : (x + 1) * a], go[x * b : (x + 1) * b]], 0)
        moved = mm(onehot, source).astype(B16)
        slab_ref[:, x] = moved.reshape(slab_ref.shape[:1] + slab_ref.shape[2:])
        outs.append(copies.start(slab_ref.at[1 - here, x], send_hbm.at[x]))
        outs.append(copies.start(slab_ref.at[here, x], own_hbm.at[x]))
    return outs


def weight_kernel(
    factor, normed_hbm, cot_hbm, att_hbm, dct_hbm, onehot_hbm, own_hbm, send_hbm,
    normed_ref, cot_ref, att_ref, dct_ref, onehot_ref, slab_ref, sems,
):
    copies = Copies(sems)
    cot_in = copies.start(cot_hbm, cot_ref)
    att_in = copies.start(att_hbm, att_ref)
    normed_in = copies.start(normed_hbm, normed_ref)
    dct_in = copies.start(dct_hbm, dct_ref)
    onehot_in = copies.start(onehot_hbm, onehot_ref)
    cot_in.wait()
    att_in.wait()
    go = (mm(cot_ref[...].T, att_ref[...]) * factor).astype(B16)
    normed_in.wait()
    dct_in.wait()
    gq = (mm(dct_ref[...], normed_ref[...]) * factor).astype(B16)
    onehot_in.wait()
    for copy in spread(copies, onehot_ref[...], gq, go, slab_ref, own_hbm, send_hbm):
        copy.wait()


def weight_slabs(factor, normed, cot, att, dct, onehot, shape):
    arrays = (normed, cot, att, dct, onehot)
    return call(
        functools.partial(weight_kernel, factor), arrays,
        (shape[1:], shape[1:]), [HBM] * 5, [HBM] * 2,
        [array.shape for array in arrays] + [shape], 5 + 2 * shape[1], 1_500_000_000,
    )


def spatial_backward_kernel(
    factor, ct_hbm, br_hbm, wo_hbm, comb_hbm, probs_hbm, tok_hbm, att_hbm, onehot_hbm,
    own_hbm, send_hbm, sg_hbm, dcomb_hbm,
    ct_ref, br_ref, wo_ref, comb_ref, probs_ref, tok_ref, att_ref, onehot_ref,
    slab_ref, sg_ref, dcomb_ref, sems,
):
    copies = Copies(sems)
    br_in = copies.start(br_hbm, br_ref)
    ct_in = copies.start(ct_hbm, ct_ref)
    wo_in = copies.start(wo_hbm, wo_ref)
    comb_in = copies.start(comb_hbm, comb_ref)
    probs_in = [copies.start(probs_hbm.at[h], probs_ref.at[h]) for h in range(HEADS)]
    tok_in = copies.start(tok_hbm, tok_ref)
    att_in = copies.start(att_hbm, att_ref)
    onehot_in = copies.start(onehot_hbm, onehot_ref)
    rows, width = ct_ref.shape
    hw = width // HEADS
    br_in.wait()
    ct_in.wait()
    branch = br_ref[...].reshape(rows, width)
    sg = (ct_ref[...].astype(F32) + branch.astype(F32)).astype(B16)
    sg_ref[...] = sg
    outs = [copies.start(sg_ref, sg_hbm)]
    wo_in.wait()
    g = mm(sg, wo_ref[...], NT).astype(B16)
    gt = g.T
    comb_in.wait()
    q = comb_ref[:, :width] * (hw ** -0.5)
    kt = comb_ref[:, width : 2 * width].T
    dqt_parts, dk_parts, dv_parts = [], [], []
    for pair in range(HEADS // 2):
        lanes = slice(pair * 2 * hw, (pair + 1) * 2 * hw)
        values = comb_ref[:, 2 * width + pair * 2 * hw : 2 * width + (pair + 1) * 2 * hw]
        dk = dv = 0.0
        for sub in range(2):
            head = 2 * pair + sub
            probs_in[head].wait()
            p = probs_ref[head]
            ds = score_back(p, mm(values, one_head(gt[lanes], sub, hw, 0)))
            dqt = mm(kt[head * hw : (head + 1) * hw], ds) * (hw ** -0.5)
            dqt_parts.append(dqt.astype(B16))
            dk = dk + mm(ds, one_head(q[:, lanes], sub, hw, 1))
            dv = dv + mm(p, one_head(g[:, lanes], sub, hw, 1))
        dk_parts.append(dk.astype(B16))
        dv_parts.append(dv.astype(B16))
    dqt = jnp.concatenate(dqt_parts, 0)
    dk = jnp.concatenate(dk_parts, 1)
    dv = jnp.concatenate(dv_parts, 1)
    tok_in.wait()
    scaled, _ = normalize(tok_ref[...].astype(F32))
    normed = scaled.astype(B16)
    dct = jnp.concatenate([dqt, dk.T, dv.T], 0)
    gq = (mm(dct, normed) * factor).astype(B16)
    att_in.wait()
    go = (mm(sg.T, att_ref[...]) * factor).astype(B16)
    onehot_in.wait()
    outs += spread(copies, onehot_ref[...], gq, go, slab_ref, own_hbm, send_hbm)
    dcomb_ref[:, :width] = dqt.T
    dcomb_ref[:, width : 2 * width] = dk
    dcomb_ref[:, 2 * width :] = dv
    outs.append(copies.start(dcomb_ref, dcomb_hbm))
    for copy in outs:
        copy.wait()


def spatial_backward(factor, ct, branch, wo, comb, probs, tokens, att, onehot, shape):
    rows, width = tokens.shape
    arrays = (ct, branch, wo, comb, probs, tokens, att, onehot)
    square, wide = (rows, width), (rows, 3 * width)
    return call(
        functools.partial(spatial_backward_kernel, factor), arrays,
        (shape[1:], shape[1:], square, wide), [HBM] * 8, [HBM] * 4,
        [array.shape for array in arrays] + [shape, square, wide],
        9 + HEADS + 2 * shape[1], 4_000_000_000,
    )


def token_kernel(
    tok_hbm, w_hbm, dcomb_hbm, sg_hbm, out_ref, tok_ref, w_ref, dcomb_ref, sg_ref, sems
):
    copies = Copies(sems)
    pending = [
        copies.start(source, target)
        for source, target in (
            (w_hbm, w_ref), (dcomb_hbm, dcomb_ref), (tok_hbm, tok_ref), (sg_hbm, sg_ref)
        )
    ]
    for copy in pending:
        copy.wait()
    scaled, inverse = normalize(tok_ref[...].astype(F32))
    u = mm(dcomb_ref[...], w_ref[...], NT)
    out_ref[...] = (sg_ref[...].astype(F32) + normalize_back(scaled, inverse, u)).astype(B16)


def token_gradient(tokens, w, dcomb, sg):
    arrays = (tokens, w, dcomb, sg)
    return call(
        token_kernel, arrays, (tokens.shape,), [HBM] * 4, [VM],
        [array.shape for array in arrays], 4, 500_000_000,
    )[0]


SEQ = (("x", 4), ("yh", 2), ("z", 8), ("core", 2))


def seq_size():
    return lax.axis_size("seq")


def place(name):
    stride = 1
    for member, size in reversed(SEQ):
        if member == name:
            return stride, size
        stride *= size


def coordinate(name):
    stride, size = place(name)
    return lax.axis_index("seq") // stride % size


def shift(array, name, step):
    stride, size = place(name)
    pairs = []
    for index in range(seq_size()):
        at = index // stride % size
        pairs.append((index, index + ((at + step) % size - at) * stride))
    return lax.ppermute(array, "seq", pairs)


def stage(chunks, name):
    size = chunks.shape[0]
    here = coordinate(name)
    total = lax.dynamic_index_in_dim(chunks, here, 0, keepdims=False).astype(F32)
    for step in range(1, size):
        part = lax.dynamic_index_in_dim(chunks, (here + step) % size, 0, keepdims=False)
        total = total + shift(part, name, step).astype(F32)
    return total


def slab_order(width):
    sizes = dict(SEQ)
    a, b = 3 * width // seq_size(), width // seq_size()
    group = seq_size() // sizes["x"]
    table = np.zeros(((a + b) * group, (a + b) * group), np.float32)
    row = 0
    for core in range(sizes["core"]):
        for z in range(sizes["z"]):
            for yh in range(sizes["yh"]):
                member = (yh * sizes["z"] + z) * sizes["core"] + core
                for i in range(a + b):
                    source = member * a + i if i < a else group * a + member * b + i - a
                    table[row, source] = 1.0
                    row += 1
    shape = (sizes["core"], sizes["x"], sizes["z"], sizes["yh"] * (a + b), width)
    return jnp.asarray(table, B16), shape


def first_stages(own, send):
    part = (own.astype(F32) + shift(send, "core", 1).astype(F32)).astype(B16)
    return stage(part, "x").astype(B16)


def groups_of(*names):
    wanted = [place(name) for name in names]
    groups = []
    for index in range(seq_size()):
        if all(index // stride % size == 0 for stride, size in wanted):
            members = [index]
            for stride, size in wanted:
                members = [at + k * stride for at in members for k in range(size)]
            groups.append(members)
    return groups


def last_stages(part):
    yh, z = part.shape[:2]
    flat = part.reshape(yh * z, *part.shape[2:])
    got = lax.all_to_all(
        flat, "seq", split_axis=0, concat_axis=0, tiled=True, axis_index_groups=groups_of("yh", "z")
    )
    mine = jnp.sum(got.astype(F32), 0).astype(B16)
    other = lax.ppermute(mine, "dp", [(0, 1), (1, 0)])
    return mine.astype(F32) + other.astype(F32)


def on_device(tokens, cotangent, wqkv_spatial, wo_spatial, wqkv_temporal, wo_temporal):
    clips, frames, patches, width = tokens.shape
    factor = (clips * frames * patches * lax.axis_size("dp") * seq_size()) ** (-0.5)
    table, slab_shape = slab_order(width)
    tok = tokens.reshape(patches, width)
    cot = cotangent.reshape(patches, width)
    traded = (seq_size(), 2 * patches // seq_size(), width)

    def trade(array):
        return lax.all_to_all(array, "seq", split_axis=0, concat_axis=0, tiled=True)

    stream, comb, att, probs = spatial_forward(tok, cot, wqkv_spatial, wo_spatial, traded)
    branch, normed_t, cot_p, att_t, dct = temporal(trade(stream), wqkv_temporal, wo_temporal)
    branch = trade(branch)
    own, send = weight_slabs(factor, normed_t, cot_p, att_t, dct, table, slab_shape)
    half_t = first_stages(own, send)
    branch, half_t = lax.optimization_barrier((branch, half_t))
    own, send, stream_grad, dcomb = spatial_backward(
        factor, cot, branch, wo_spatial, comb, probs, tok, att, table, slab_shape
    )
    half_s = first_stages(own, send)
    token_grad = token_gradient(tok, wqkv_spatial, dcomb, stream_grad)
    z, rows = half_s.shape[:2]
    joined = jnp.concatenate(
        [
            jnp.moveaxis(half.reshape(z, 2, rows // 2, width), 1, 0)
            for half in (half_s, half_t)
        ],
        2,
    )
    own = last_stages(joined)
    a, b = 3 * width // seq_size(), width // seq_size()
    shares = (own[:a].T, own[a : a + b].T, own[a + b : 2 * a + b].T, own[2 * a + b :].T)
    return (token_grad.reshape(tokens.shape), *shares)


def solution(mesh):
    in_specs = (P("dp", "seq", None, None), P("dp", "seq", None, None), P(), P(), P(), P())
    out_specs = (
        P("dp", "seq", None, None),
        P(None, "seq"),
        P(None, "seq"),
        P(None, "seq"),
        P(None, "seq"),
    )
    return jax.shard_map(
        on_device, mesh=mesh, in_specs=in_specs, out_specs=out_specs, check_vma=False
    )
```

profile of v0, /device:TPU:8, one launch (start us, length us, event | category | flops | bytes accessed | tf_op | source)
XLA Modules:
  0.0 140.1 jit_solution(1215161158830780341)
XLA Ops:
  0.6 7.1 %shard_map.110 = (bf16[128,8,384]{2,1,0:T(8,128)(2,1)}, bf16[512,1152]{1,0:T(8,128)(2,1)}, bf16[512,384]{1,0:T(8,128)(2,1)}, bf16[6,512,512]{2,1,0:T(8,128)(2,1)}) custom-call(bf16[512,384]{1,0:T(8,128)(2,1)} %bitcast.39, bf16[512,384]{1,0:T(8,128)(2,1)} %bitcast.43, bf16[384,1152]{1,0:T(8,128)(2,1)} %w_hbm.5, bf16[384,384]{1,0:T(8,128)(2,1)} %wo_hbm.5), custom_call_target="tpu_custom_call" | custom-call | flops 2000000000 | bytes 1966080 | tf_op jit(solution)/shard_map/pallas_call | solution.py:73
  7.7 40.2 %all_to_all.15.slab_ref = bf16[128,8,384]{2,1,0:T(8,128)(2,1)} all-to-all(bf16[128,8,384]{2,1,0:T(8,128)(2,1)} %get-tuple-element.22), channel_id=1, replica_groups=mesh['dp'=2,'seq'=128] {'seq'}, dimensions={0} | all-to-all | bytes 1572864 | tf_op jit(solution)/shard_map/all_to_all | solution.py:477
  47.9 10.3 %shard_map.111 = (bf16[128,4,384]{2,1,0:T(4,128)(2,1)}, bf16[512,384]{1,0:T(8,128)(2,1)}, bf16[512,384]{1,0:T(8,128)(2,1)}, bf16[512,384]{1,0:T(8,128)(2,1)}, bf16[1152,512]{1,0:T(8,128)(2,1)}) custom-call(bf16[128,8,384]{2,1,0:T(8,128)(2,1)} %all_to_all.15.slab_ref, bf16[384,1152]{1,0:T(8,128)(2,1)} %w_hbm.4, bf16[384,384]{1,0:T(8,128)(2,1)} %wo_hbm.4), custom_call_target="tpu_custom_call" | custom-call | flops 3000000000 | bytes 1966080 | tf_op jit(solution)/shard_map/pallas_call | solution.py:73
  58.2 4.1 %shard_map.112 = (bf16[4,8,24,384]{3,2,1,0:T(8,128)(2,1)}, bf16[4,8,24,384]{3,2,1,0:T(8,128)(2,1)}) custom-call(bf16[512,384]{1,0:T(8,128)(2,1)} %get-tuple-element.24.normed_hbm, bf16[512,384]{1,0:T(8,128)(2,1)} %get-tuple-element.25.cot_hbm, bf16[512,384]{1,0:T(8,128)(2,1)} %get-tuple-element.26.att_hbm, bf16[1152,512]{1,0:T(8,128)(2,1)} %get-tuple-element.27.dct_hbm, ...), custom_call_target="tpu_custom_call" | custom-call | flops 1500000000 | bytes 2654208 | tf_op jit(solution)/shard_map/pallas_call | solution.py:73
  62.3 1.4 collective-permute-start
  63.7 6.2 %all-to-all-start.1 = ((bf16[128,4,384]{2,1,0:T(4,128)(2,1)}), bf16[128,4,384]{2,1,0:T(4,128)(2,1)S(1)}, u32[]{:S(2)}, u32[]{:S(2)}) async-start(bf16[128,4,384]{2,1,0:T(4,128)(2,1)} %get-tuple-element.23), calls=%async_computation.1 | async-start | bytes 786432 | tf_op jit(solution)/shard_map/all_to_all | solution.py:477
  70.2 3.0 %collective-permute-start.3 = (bf16[8,24,384]{2,1,0:T(8,128)(2,1)S(1)}, bf16[8,24,384]{2,1,0:T(8,128)(2,1)S(1)}, u32[]{:S(2)}, u32[]{:S(2)}) collective-permute-start(bf16[8,24,384]{2,1,0:T(8,128)(2,1)S(1)} %get-tuple-element.43), channel_id=1, source_target_pairs={{0,96},{1,97},{2,98},{3,99},{4,100},{5,101},{6,102},{7,103},{8,104... | collective-permute-start | bytes 442376 | tf_op jit(solution)/shard_map/ppermute | solution.py:409
  73.5 1.1 collective-permute-start.1
  74.6 8.1 %collective-permute-done.3 = bf16[8,24,384]{2,1,0:T(8,128)(2,1)S(1)} collective-permute-done((bf16[8,24,384]{2,1,0:T(8,128)(2,1)S(1)}, bf16[8,24,384]{2,1,0:T(8,128)(2,1)S(1)}, u32[]{:S(2)}, u32[]{:S(2)}) %collective-permute-start.3) | collective-permute-done | bytes 147488 | tf_op jit(solution)/shard_map/ppermute | solution.py:409
  82.7 0.8 collective-permute-done.2
  83.5 2.6 %collective-permute-done.1 = bf16[8,24,384]{2,1,0:T(8,128)(2,1)S(1)} collective-permute-done((bf16[8,24,384]{2,1,0:T(8,128)(2,1)S(1)}, bf16[8,24,384]{2,1,0:T(8,128)(2,1)S(1)}, u32[]{:S(2)}, u32[]{:S(2)}) %collective-permute-start.1) | collective-permute-done | bytes 147488 | tf_op jit(solution)/shard_map/ppermute | solution.py:409
  86.2 1.8 %all-to-all-done.1.br_hbm = bf16[128,4,384]{2,1,0:T(4,128)(2,1)S(1)} async-done(((bf16[128,4,384]{2,1,0:T(4,128)(2,1)}), bf16[128,4,384]{2,1,0:T(4,128)(2,1)S(1)}, u32[]{:S(2)}, u32[]{:S(2)}) %all-to-all-start.1) | async-done | bytes 393248 | tf_op jit(solution)/shard_map/all_to_all | solution.py:477
  88.0 0.8 copy-done.1
  88.8 11.4 %shard_map.113 = (bf16[4,8,24,384]{3,2,1,0:T(8,128)(2,1)}, bf16[4,8,24,384]{3,2,1,0:T(8,128)(2,1)}, bf16[512,384]{1,0:T(8,128)(2,1)}, bf16[512,1152]{1,0:T(8,128)(2,1)}) custom-call(bf16[512,384]{1,0:T(8,128)(2,1)} %bitcast.44, bf16[128,4,384]{2,1,0:T(4,128)(2,1)} %copy-done.1, bf16[384,384]{1,0:T(8,128)(2,1)} %wo_hbm.5, ...), custom_call_target="tpu_custom_call" | custom-call | flops 4000000000 | bytes 6488064 | tf_op jit(solution)/shard_map/pallas_call | solution.py:73
  100.6 1.9 %collective-permute-done.4 = bf16[4,8,24,384]{3,2,1,0:T(8,128)(2,1)S(1)} collective-permute-done((bf16[4,8,24,384]{3,2,1,0:T(8,128)(2,1)}, bf16[4,8,24,384]{3,2,1,0:T(8,128)(2,1)S(1)}, u32[]{:S(2)}, u32[]{:S(2)}) %collective-permute-start.4) | collective-permute-done | bytes 589856 | tf_op jit(solution)/shard_map/ppermute | solution.py:409
  102.5 1.2 add_convert_fusion
  103.8 1.0 collective-permute-start.7
  104.8 1.9 %collective-permute-start.6 = (bf16[8,24,384]{2,1,0:T(8,128)(2,1)S(1)}, bf16[8,24,384]{2,1,0:T(8,128)(2,1)S(1)}, u32[]{:S(2)}, u32[]{:S(2)}) collective-permute-start(bf16[8,24,384]{2,1,0:T(8,128)(2,1)S(1)} %get-tuple-element.41), channel_id=1, source_target_pairs={{0,64},{1,65},{2,66},{3,67},{4,68},{5,69},{6,70},{7,71},{8,72},{9,... | collective-permute-start | bytes 442376 | tf_op jit(solution)/shard_map/ppermute | solution.py:409
  106.7 3.9 %collective-permute-done.7 = bf16[8,24,384]{2,1,0:T(8,128)(2,1)S(1)} collective-permute-done((bf16[8,24,384]{2,1,0:T(8,128)(2,1)S(1)}, bf16[8,24,384]{2,1,0:T(8,128)(2,1)S(1)}, u32[]{:S(2)}, u32[]{:S(2)}) %collective-permute-start.7) | collective-permute-done | bytes 147488 | tf_op jit(solution)/shard_map/ppermute | solution.py:409
  110.6 2.4 %collective-permute-done.6 = bf16[8,24,384]{2,1,0:T(8,128)(2,1)S(1)} collective-permute-done((bf16[8,24,384]{2,1,0:T(8,128)(2,1)S(1)}, bf16[8,24,384]{2,1,0:T(8,128)(2,1)S(1)}, u32[]{:S(2)}, u32[]{:S(2)}) %collective-permute-start.6) | collective-permute-done | bytes 147488 | tf_op jit(solution)/shard_map/ppermute | solution.py:409
  113.0 2.1 %collective-permute-done.5 = bf16[8,24,384]{2,1,0:T(8,128)(2,1)S(1)} collective-permute-done((bf16[8,24,384]{2,1,0:T(8,128)(2,1)S(1)}, bf16[8,24,384]{2,1,0:T(8,128)(2,1)S(1)}, u32[]{:S(2)}, u32[]{:S(2)}) %collective-permute-start.5) | collective-permute-done | bytes 147488 | tf_op jit(solution)/shard_map/ppermute | solution.py:409
  115.4 18.5 %all_to_all.16 = bf16[16,24,384]{2,1,0:T(8,128)(2,1)S(1)} all-to-all(bf16[16,24,384]{2,1,0:T(8,128)(2,1)S(1)} %bitcast.36), channel_id=1, replica_groups={{0,2,4,6,8,10,12,14,16,18,20,22,24,26,28,30},{1,3,5,7,9,11,13,15,17,19,..., dimensions={0} | all-to-all | bytes 589824 | tf_op jit(solution)/shard_map/all_to_all | solution.py:460
  133.9 1.4 %collective-permute-start.8 = (bf16[24,384]{1,0:T(8,128)(2,1)S(1)}, bf16[24,384]{1,0:T(8,128)(2,1)S(1)}, u32[]{:S(2)}, u32[]{:S(2)}) collective-permute-start(bf16[24,384]{1,0:T(8,128)(2,1)S(1)} %reduce_sum.12), channel_id=1, source_target_pairs={{0,128},{128,0},{1,129},{129,1},{2,130},{130,2},{3,131},{131,3},{4... | collective-permute-start | bytes 55304 | tf_op jit(solution)/shard_map/ppermute | solution.py:464
  135.3 3.6 %shard_map.114 = bf16[512,384]{1,0:T(8,128)(2,1)} custom-call(bf16[512,384]{1,0:T(8,128)(2,1)} %bitcast.41, bf16[384,1152]{1,0:T(8,128)(2,1)} %w_hbm.5, bf16[512,1152]{1,0:T(8,128)(2,1)} %get-tuple-element.34.dcomb_hbm, bf16[512,384]{1,0:T(8,128)(2,1)} %get-tuple-element.35.sg_hbm), custom_call_target="tpu_custom_call" | custom-call | flops 500000000 | bytes 2850816 | tf_op jit(solution)/shard_map/pallas_call | solution.py:73
  (21 shorter events, 2.6 us)
Async XLA Ops:
  62.3 7.6 %copy-start = (bf16[4,8,24,384]{3,2,1,0:T(8,128)(2,1)S(1)}, bf16[4,8,24,384]{3,2,1,0:T(8,128)(2,1)}, u32[]{:S(2)}) copy-start(bf16[4,8,24,384]{3,2,1,0:T(8,128)(2,1)} %get-tuple-element.28) | copy-start | bytes 1769476
  62.3 7.6 %collective-permute-start = (bf16[4,8,24,384]{3,2,1,0:T(8,128)(2,1)}, bf16[4,8,24,384]{3,2,1,0:T(8,128)(2,1)S(1)}, u32[]{:S(2)}, u32[]{:S(2)}) collective-permute-start(bf16[4,8,24,384]{3,2,1,0:T(8,128)(2,1)} %get-tuple-element.29), channel_id=1, source_target_pairs={{0,1},{1,0},{2,3},{3,2},{4,5},{5,4},{6,7},{7,6},{8,9},{9,8},{10,11... | collective-permute-start | bytes 1769480 | tf_op jit(solution)/shard_map/ppermute | solution.py:409
  63.7 24.3 %all-to-all-start.1 = ((bf16[128,4,384]{2,1,0:T(4,128)(2,1)}), bf16[128,4,384]{2,1,0:T(4,128)(2,1)S(1)}, u32[]{:S(2)}, u32[]{:S(2)}) async-start(bf16[128,4,384]{2,1,0:T(4,128)(2,1)} %get-tuple-element.23), calls=%async_computation.1 | async-start | bytes 786432 | tf_op jit(solution)/shard_map/all_to_all | solution.py:477
  70.2 12.5 %collective-permute-start.3 = (bf16[8,24,384]{2,1,0:T(8,128)(2,1)S(1)}, bf16[8,24,384]{2,1,0:T(8,128)(2,1)S(1)}, u32[]{:S(2)}, u32[]{:S(2)}) collective-permute-start(bf16[8,24,384]{2,1,0:T(8,128)(2,1)S(1)} %get-tuple-element.43), channel_id=1, source_target_pairs={{0,96},{1,97},{2,98},{3,99},{4,100},{5,101},{6,102},{7,103},{8,104... | collective-permute-start | bytes 442376 | tf_op jit(solution)/shard_map/ppermute | solution.py:409
  73.1 10.4 %collective-permute-start.2 = (bf16[8,24,384]{2,1,0:T(8,128)(2,1)S(1)}, bf16[8,24,384]{2,1,0:T(8,128)(2,1)S(1)}, u32[]{:S(2)}, u32[]{:S(2)}) collective-permute-start(bf16[8,24,384]{2,1,0:T(8,128)(2,1)S(1)} %get-tuple-element.44), channel_id=1, source_target_pairs={{0,64},{1,65},{2,66},{3,67},{4,68},{5,69},{6,70},{7,71},{8,72},{9,... | collective-permute-start | bytes 442376 | tf_op jit(solution)/shard_map/ppermute | solution.py:409
  73.5 12.6 %collective-permute-start.1 = (bf16[8,24,384]{2,1,0:T(8,128)(2,1)S(1)}, bf16[8,24,384]{2,1,0:T(8,128)(2,1)S(1)}, u32[]{:S(2)}, u32[]{:S(2)}) collective-permute-start(bf16[8,24,384]{2,1,0:T(8,128)(2,1)S(1)} %get-tuple-element.42), channel_id=1, source_target_pairs={{0,32},{1,33},{2,34},{3,35},{4,36},{5,37},{6,38},{7,39},{8,40},{9,... | collective-permute-start | bytes 442376 | tf_op jit(solution)/shard_map/ppermute | solution.py:409
  88.0 0.8 copy-start.1
  100.2 2.3 %collective-permute-start.4 = (bf16[4,8,24,384]{3,2,1,0:T(8,128)(2,1)}, bf16[4,8,24,384]{3,2,1,0:T(8,128)(2,1)S(1)}, u32[]{:S(2)}, u32[]{:S(2)}) collective-permute-start(bf16[4,8,24,384]{3,2,1,0:T(8,128)(2,1)} %get-tuple-element.37), channel_id=1, source_target_pairs={{0,1},{1,0},{2,3},{3,2},{4,5},{5,4},{6,7},{7,6},{8,9},{9,8},{10,11... | collective-permute-start | bytes 1769480 | tf_op jit(solution)/shard_map/ppermute | solution.py:409
  103.8 6.8 %collective-permute-start.7 = (bf16[8,24,384]{2,1,0:T(8,128)(2,1)S(1)}, bf16[8,24,384]{2,1,0:T(8,128)(2,1)S(1)}, u32[]{:S(2)}, u32[]{:S(2)}) collective-permute-start(bf16[8,24,384]{2,1,0:T(8,128)(2,1)S(1)} %get-tuple-element.40), channel_id=1, source_target_pairs={{0,96},{1,97},{2,98},{3,99},{4,100},{5,101},{6,102},{7,103},{8,104... | collective-permute-start | bytes 442376 | tf_op jit(solution)/shard_map/ppermute | solution.py:409
  104.8 8.2 %collective-permute-start.6 = (bf16[8,24,384]{2,1,0:T(8,128)(2,1)S(1)}, bf16[8,24,384]{2,1,0:T(8,128)(2,1)S(1)}, u32[]{:S(2)}, u32[]{:S(2)}) collective-permute-start(bf16[8,24,384]{2,1,0:T(8,128)(2,1)S(1)} %get-tuple-element.41), channel_id=1, source_target_pairs={{0,64},{1,65},{2,66},{3,67},{4,68},{5,69},{6,70},{7,71},{8,72},{9,... | collective-permute-start | bytes 442376 | tf_op jit(solution)/shard_map/ppermute | solution.py:409
  106.7 8.5 %collective-permute-start.5 = (bf16[8,24,384]{2,1,0:T(8,128)(2,1)S(1)}, bf16[8,24,384]{2,1,0:T(8,128)(2,1)S(1)}, u32[]{:S(2)}, u32[]{:S(2)}) collective-permute-start(bf16[8,24,384]{2,1,0:T(8,128)(2,1)S(1)} %get-tuple-element.39), channel_id=1, source_target_pairs={{0,32},{1,33},{2,34},{3,35},{4,36},{5,37},{6,38},{7,39},{8,40},{9,... | collective-permute-start | bytes 442376 | tf_op jit(solution)/shard_map/ppermute | solution.py:409
  133.9 5.0 %collective-permute-start.8 = (bf16[24,384]{1,0:T(8,128)(2,1)S(1)}, bf16[24,384]{1,0:T(8,128)(2,1)S(1)}, u32[]{:S(2)}, u32[]{:S(2)}) collective-permute-start(bf16[24,384]{1,0:T(8,128)(2,1)S(1)} %reduce_sum.12), channel_id=1, source_target_pairs={{0,128},{128,0},{1,129},{129,1},{2,130},{130,2},{3,131},{131,3},{4... | collective-permute-start | bytes 55304 | tf_op jit(solution)/shard_map/ppermute | solution.py:464
where the time goes:
time: 141 us; the launch traced here: 140 us
  blocking collectives  58.6 us (42%)
  Pallas kernels  36.5 us (26%)
  waiting for transfers between devices  23.7 us (17%)
  starting transfers between devices  16.7 us (12%)
  local copies, waits for them, and re-layouts  2.17 us (2%)
  other arithmetic  1.61 us (1%)
    all_to_all x1, blocking collectives, trade(): return lax.all_to_all(array, 'seq', split_axis=0, concat_axis=0, tiled=True)  40.2 us
    pallas_call x5, Pallas kernels, call(): pl.pallas_call(kernel, out_shape=tuple((jax.ShapeDtypeStruct(shape, B16)...  36.5 us
    ppermute x8, waiting for transfers between devices, shift(): return lax.ppermute(array, 'seq', pairs)  21.9 us
    all_to_all x1, blocking collectives, last_stages(): lax.all_to_all(flat, 'seq', split_axis=0, concat_axis=0, tiled=True, axis...  18.5 us
    ppermute x8, starting transfers between devices, shift(): return lax.ppermute(array, 'seq', pairs)  9.12 us
    all_to_all x1, starting transfers between devices, trade(): return lax.all_to_all(array, 'seq', split_axis=0, concat_axis=0, tiled=True)  6.17 us
  transfers between devices with their start and end apart: 10, of which 8 were waited for; matrix products, arithmetic and copies ran while one was open for 0% of the time, Pallas kernels for 3%

commit v1 on v0

--- a/solution.py
+++ b/solution.py
@@ -69,7 +69,7 @@
 HBM = pl.BlockSpec(memory_space=pltpu.HBM)
 
 
-def call(kernel, arrays, outs, in_specs, out_specs, scratch, copies, flops, exps=0):
+def call(kernel, arrays, outs, in_specs, out_specs, scratch, copies, flops, exps=0, limit=None):
     return pl.pallas_call(
         kernel,
         out_shape=tuple(jax.ShapeDtypeStruct(shape, B16) for shape in outs),
@@ -77,6 +77,7 @@
         out_specs=tuple(out_specs),
         scratch_shapes=[pltpu.VMEM(shape, B16) for shape in scratch]
         + [pltpu.SemaphoreType.DMA((copies,))],
+        compiler_params=pltpu.CompilerParams(vmem_limit_bytes=limit and limit << 20),
         cost_estimate=pl.CostEstimate(
             flops=flops,
             bytes_accessed=sum(array.size * 2 for array in arrays),
@@ -97,8 +98,8 @@
 
 
 def spatial_forward_kernel(
-    tok_hbm, cot_hbm, w_hbm, wo_hbm, slab_ref, comb_hbm, att_hbm, probs_hbm,
-    tok_ref, cot_ref, w_ref, wo_ref, comb_ref, att_ref, probs_ref, sems,
+    tok_hbm, cot_hbm, w_hbm, wo_hbm, slab_ref, saved_hbm,
+    tok_ref, cot_ref, w_ref, wo_ref, wide_ref, probs_ref, sems,
 ):
     copies = Copies(sems)
     tok_in = copies.start(tok_hbm, tok_ref)
@@ -113,8 +114,12 @@
     scaled, _ = normalize(x)
     w_in.wait()
     comb = mm(scaled.astype(B16), w_ref[...]).astype(B16)
-    comb_ref[...] = comb
-    outs.append(copies.start(comb_ref, comb_hbm))
+    wide_ref[:, : 3 * width] = comb
+    rows = comb.shape[0]
+    for part in range(2):
+        outs.append(
+            copies.start(wide_ref.at[:, part * rows : (part + 1) * rows], saved_hbm.at[HEADS + part])
+        )
     qt = (comb[:, :width] * (hw ** -0.5)).T
     vt = comb[:, 2 * width :].T
     parts = []
@@ -125,11 +130,11 @@
             head = 2 * pair + sub
             p = softmax_rows(mm(keys, one_head(qt[at : at + 2 * hw], sub, hw, 0)))
             probs_ref[head] = p
-            outs.append(copies.start(probs_ref.at[head], probs_hbm.at[head]))
+            outs.append(copies.start(probs_ref.at[head], saved_hbm.at[head]))
             parts.append(mm(vt[head * hw : (head + 1) * hw], p).astype(B16))
     att = jnp.concatenate(parts, 0).T
-    att_ref[...] = att
-    outs.append(copies.start(att_ref, att_hbm))
+    wide_ref[:, 3 * width :] = att
+    outs.append(copies.start(wide_ref.at[:, 2 * rows :], saved_hbm.at[HEADS + 2]))
     wo_in.wait()
     out = (x + mm(att, wo_ref[...])).astype(B16)
     cot_in.wait()
@@ -141,23 +146,18 @@
 
 def spatial_forward(tokens, cotangent, w, wo, slab):
     rows, width = tokens.shape
-    wide, square = (rows, 3 * width), (rows, width)
-    probs = (HEADS, rows, rows)
+    wide, square = (rows, 4 * width), (rows, width)
     return call(
         spatial_forward_kernel, (tokens, cotangent, w, wo),
-        (slab, wide, square, probs), [HBM] * 4, [VM] + [HBM] * 3,
-        [square, square, w.shape, wo.shape, wide, square, probs],
-        6 + HEADS, 2_000_000_000, 1_600_000,
+        (slab, (HEADS + 3, rows, rows)), [HBM] * 4, [VM, HBM],
+        [square, square, w.shape, wo.shape, wide, (HEADS, rows, rows)],
+        7 + HEADS, 2_000_000_000, 1_600_000, None,
     )
 
 
 def temporal_kernel(
-    slab_ref, w_hbm, wo_hbm, branch_ref, normed_hbm, cot_hbm, att_hbm, dct_hbm,
-    w_ref, wo_ref, normed_ref, cot_ref, att_ref, dct_ref, sems,
+    factor, slab_ref, w_ref, wo_ref, branch_ref, normed_ref, go_ref, dct_ref, _,
 ):
-    copies = Copies(sems)
-    w_in = copies.start(w_hbm, w_ref)
-    wo_in = copies.start(wo_hbm, wo_ref)
     frames, both, width = slab_ref.shape
     patches = both // 2
     rows = frames * patches
@@ -166,15 +166,10 @@
     slab = slab_ref[...]
     x = mm(gather, slab[:, :patches].reshape(rows, width))
     cot = mm(gather, slab[:, patches:].reshape(rows, width)).astype(B16)
-    cot_ref[...] = cot
-    outs = [copies.start(cot_ref, cot_hbm)]
     scaled, inverse = normalize(x)
     normed = scaled.astype(B16)
     normed_ref[...] = normed
-    outs.append(copies.start(normed_ref, normed_hbm))
-    w_in.wait()
     comb = mm(normed, w_ref[...]).astype(B16)
-    wo_in.wait()
     g = mm(cot, wo_ref[...], NT).astype(B16)
     q = comb[:, :width] * (hw ** -0.5)
     k = comb[:, width : 2 * width]
@@ -201,14 +196,13 @@
         dk_parts.append(jnp.concatenate(dk_p, 1))
         dv_parts.append(jnp.concatenate(dv_p, 1))
     dqt = jnp.concatenate(dqt_parts, 1)
-    att_ref[...] = jnp.concatenate(att_parts, 1).T
-    outs.append(copies.start(att_ref, att_hbm))
+    att = jnp.concatenate(att_parts, 1).T
+    go_ref[...] = (mm(cot.T, att) * factor).astype(B16)
     dk = jnp.concatenate(dk_parts, 0)
     dv = jnp.concatenate(dv_parts, 0)
     dct_ref[:width] = dqt
     dct_ref[width : 2 * width] = dk.T
     dct_ref[2 * width :] = dv.T
-    outs.append(copies.start(dct_ref, dct_hbm))
     u = (
         mm(dqt.T, w_ref[:, :width], NT)
         + mm(dk, w_ref[:, width : 2 * width], NT)
@@ -217,94 +211,64 @@
     branch = normalize_back(scaled, inverse, u).astype(B16)
     scatter = regroup(rows, patches, frames)
     branch_ref[...] = mm(scatter, branch).astype(B16).reshape(branch_ref.shape)
-    for copy in outs:
-        copy.wait()
-
-
-def temporal(slab, w, wo):
+
+
+def temporal(factor, slab, w, wo):
     frames, both, width = slab.shape
     rows = frames * both // 2
-    square = (rows, width)
     return call(
-        temporal_kernel, (slab, w, wo),
-        ((frames, both // 2, width), square, square, square, (3 * width, rows)),
-        [VM, HBM, HBM], [VM] + [HBM] * 4,
-        [w.shape, wo.shape, square, square, square, (3 * width, rows)],
-        6, 3_000_000_000, 400_000,
-    )
-
-
-def spread(copies, onehot, gq, go, slab_ref, own_hbm, send_hbm):
+        functools.partial(temporal_kernel, factor), (slab, w, wo),
+        ((frames, both // 2, width), (rows, width), wo.shape, (3 * width, rows)),
+        [VM] * 3, [VM] * 4, [], 1, 3_000_000_000, 400_000, 48,
+    )
+
+
+def spread(onehot, gq, go, slab_ref, own_ref, send_ref):
     here = lax.axis_index("seq") % slab_ref.shape[0]
     groups = slab_ref.shape[1]
     a, b = gq.shape[0] // groups, go.shape[0] // groups
-    outs = []
     for x in range(groups):
         source = jnp.concatenate([gq[x * a : (x + 1) * a], go[x * b : (x + 1) * b]], 0)
         moved = mm(onehot, source).astype(B16)
         slab_ref[:, x] = moved.reshape(slab_ref.shape[:1] + slab_ref.shape[2:])
-        outs.append(copies.start(slab_ref.at[1 - here, x], send_hbm.at[x]))
-        outs.append(copies.start(slab_ref.at[here, x], own_hbm.at[x]))
-    return outs
-
-
-def weight_kernel(
-    factor, normed_hbm, cot_hbm, att_hbm, dct_hbm, onehot_hbm, own_hbm, send_hbm,
-    normed_ref, cot_ref, att_ref, dct_ref, onehot_ref, slab_ref, sems,
+        send_ref[x] = slab_ref[1 - here, x]
+        own_ref[x] = slab_ref[here, x]
+
+
+def weight_kernel(factor, normed_ref, go_ref, dct_ref, onehot_ref, own_ref, send_ref, slab_ref, _):
+    gq = (mm(dct_ref[...], normed_ref[...]) * factor).astype(B16)
+    spread(onehot_ref[...], gq, go_ref[...], slab_ref, own_ref, send_ref)
+
+
+def weight_slabs(factor, normed, go, dct, onehot, shape):
+    return call(
+        functools.partial(weight_kernel, factor), (normed, go, dct, onehot),
+        (shape[1:], shape[1:]), [VM] * 4, [VM] * 2, [shape], 1, 1_500_000_000, 0, 48,
+    )
+
+
+def spatial_backward_kernel(
+    factor, ct_ref, br_ref, wo_ref, saved_hbm, tok_ref, onehot_ref,
+    own_ref, send_ref, sg_ref, dcomb_ref,
+    comb_ref, probs_ref, slab_ref, sems,
 ):
     copies = Copies(sems)
-    cot_in = copies.start(cot_hbm, cot_ref)
-    att_in = copies.start(att_hbm, att_ref)
-    normed_in = copies.start(normed_hbm, normed_ref)
-    dct_in = copies.start(dct_hbm, dct_ref)
-    onehot_in = copies.start(onehot_hbm, onehot_ref)
-    cot_in.wait()
-    att_in.wait()
-    go = (mm(cot_ref[...].T, att_ref[...]) * factor).astype(B16)
-    normed_in.wait()
-    dct_in.wait()
-    gq = (mm(dct_ref[...], normed_ref[...]) * factor).astype(B16)
-    onehot_in.wait()
-    for copy in spread(copies, onehot_ref[...], gq, go, slab_ref, own_hbm, send_hbm):
-        copy.wait()
-
-
-def weight_slabs(factor, normed, cot, att, dct, onehot, shape):
-    arrays = (normed, cot, att, dct, onehot)
-    return call(
-        functools.partial(weight_kernel, factor), arrays,
-        (shape[1:], shape[1:]), [HBM] * 5, [HBM] * 2,
-        [array.shape for array in arrays] + [shape], 5 + 2 * shape[1], 1_500_000_000,
-    )
-
-
-def spatial_backward_kernel(
-    factor, ct_hbm, br_hbm, wo_hbm, comb_hbm, probs_hbm, tok_hbm, att_hbm, onehot_hbm,
-    own_hbm, send_hbm, sg_hbm, dcomb_hbm,
-    ct_ref, br_ref, wo_ref, comb_ref, probs_ref, tok_ref, att_ref, onehot_ref,
-    slab_ref, sg_ref, dcomb_ref, sems,
-):
-    copies = Copies(sems)
-    br_in = copies.start(br_hbm, br_ref)
-    ct_in = copies.start(ct_hbm, ct_ref)
-    wo_in = copies.start(wo_hbm, wo_ref)
-    comb_in = copies.start(comb_hbm, comb_ref)
-    probs_in = [copies.start(probs_hbm.at[h], probs_ref.at[h]) for h in range(HEADS)]
-    tok_in = copies.start(tok_hbm, tok_ref)
-    att_in = copies.start(att_hbm, att_ref)
-    onehot_in = copies.start(onehot_hbm, onehot_ref)
     rows, width = ct_ref.shape
+    comb_in = [
+        copies.start(saved_hbm.at[HEADS + part], comb_ref.at[:, part * rows : (part + 1) * rows])
+        for part in (2, 0, 1)
+    ]
+    probs_in = [copies.start(saved_hbm.at[h], probs_ref.at[h]) for h in range(HEADS)]
     hw = width // HEADS
-    br_in.wait()
-    ct_in.wait()
     branch = br_ref[...].reshape(rows, width)
     sg = (ct_ref[...].astype(F32) + branch.astype(F32)).astype(B16)
     sg_ref[...] = sg
-    outs = [copies.start(sg_ref, sg_hbm)]
-    wo_in.wait()
     g = mm(sg, wo_ref[...], NT).astype(B16)
     gt = g.T
-    comb_in.wait()
+    scaled, _ = normalize(tok_ref[...].astype(F32))
+    normed = scaled.astype(B16)
+    for copy in comb_in:
+        copy.wait()
     q = comb_ref[:, :width] * (hw ** -0.5)
     kt = comb_ref[:, width : 2 * width].T
     dqt_parts, dk_parts, dv_parts = [], [], []
@@ -326,57 +290,37 @@
     dqt = jnp.concatenate(dqt_parts, 0)
     dk = jnp.concatenate(dk_parts, 1)
     dv = jnp.concatenate(dv_parts, 1)
-    tok_in.wait()
-    scaled, _ = normalize(tok_ref[...].astype(F32))
-    normed = scaled.astype(B16)
     dct = jnp.concatenate([dqt, dk.T, dv.T], 0)
     gq = (mm(dct, normed) * factor).astype(B16)
-    att_in.wait()
-    go = (mm(sg.T, att_ref[...]) * factor).astype(B16)
-    onehot_in.wait()
-    outs += spread(copies, onehot_ref[...], gq, go, slab_ref, own_hbm, send_hbm)
+    go = (mm(sg.T, comb_ref[:, 3 * width :]) * factor).astype(B16)
+    spread(onehot_ref[...], gq, go, slab_ref, own_ref, send_ref)
     dcomb_ref[:, :width] = dqt.T
     dcomb_ref[:, width : 2 * width] = dk
     dcomb_ref[:, 2 * width :] = dv
-    outs.append(copies.start(dcomb_ref, dcomb_hbm))
-    for copy in outs:
-        copy.wait()
-
-
-def spatial_backward(factor, ct, branch, wo, comb, probs, tokens, att, onehot, shape):
+
+
+def spatial_backward(factor, ct, branch, wo, saved, tokens, onehot, shape):
     rows, width = tokens.shape
-    arrays = (ct, branch, wo, comb, probs, tokens, att, onehot)
+    arrays = (ct, branch, wo, saved, tokens, onehot)
     square, wide = (rows, width), (rows, 3 * width)
     return call(
         functools.partial(spatial_backward_kernel, factor), arrays,
-        (shape[1:], shape[1:], square, wide), [HBM] * 8, [HBM] * 4,
-        [array.shape for array in arrays] + [shape, square, wide],
-        9 + HEADS + 2 * shape[1], 4_000_000_000,
-    )
-
-
-def token_kernel(
-    tok_hbm, w_hbm, dcomb_hbm, sg_hbm, out_ref, tok_ref, w_ref, dcomb_ref, sg_ref, sems
-):
-    copies = Copies(sems)
-    pending = [
-        copies.start(source, target)
-        for source, target in (
-            (w_hbm, w_ref), (dcomb_hbm, dcomb_ref), (tok_hbm, tok_ref), (sg_hbm, sg_ref)
-        )
-    ]
-    for copy in pending:
-        copy.wait()
+        (shape[1:], shape[1:], square, wide),
+        [VM, VM, VM, HBM, VM, VM], [VM] * 4,
+        [(rows, 4 * width), (HEADS, rows, rows), shape], 3 + HEADS, 4_000_000_000, 0, 48,
+    )
+
+
+def token_kernel(tok_ref, w_ref, dcomb_ref, sg_ref, out_ref, _):
     scaled, inverse = normalize(tok_ref[...].astype(F32))
     u = mm(dcomb_ref[...], w_ref[...], NT)
     out_ref[...] = (sg_ref[...].astype(F32) + normalize_back(scaled, inverse, u)).astype(B16)
 
 
 def token_gradient(tokens, w, dcomb, sg):
-    arrays = (tokens, w, dcomb, sg)
     return call(
-        token_kernel, arrays, (tokens.shape,), [HBM] * 4, [VM],
-        [array.shape for array in arrays], 4, 500_000_000,
+        token_kernel, (tokens, w, dcomb, sg), (tokens.shape,),
+        [VM] * 4, [VM], [], 1, 500_000_000, 0, 48,
     )[0]
 
 
@@ -476,14 +420,13 @@
     def trade(array):
         return lax.all_to_all(array, "seq", split_axis=0, concat_axis=0, tiled=True)
 
-    stream, comb, att, probs = spatial_forward(tok, cot, wqkv_spatial, wo_spatial, traded)
-    branch, normed_t, cot_p, att_t, dct = temporal(trade(stream), wqkv_temporal, wo_temporal)
+    stream, saved = spatial_forward(tok, cot, wqkv_spatial, wo_spatial, traded)
+    branch, normed_t, go_t, dct = temporal(factor, trade(stream), wqkv_temporal, wo_temporal)
     branch = trade(branch)
-    own, send = weight_slabs(factor, normed_t, cot_p, att_t, dct, table, slab_shape)
+    own, send = weight_slabs(factor, normed_t, go_t, dct, table, slab_shape)
     half_t = first_stages(own, send)
-    branch, half_t = lax.optimization_barrier((branch, half_t))
     own, send, stream_grad, dcomb = spatial_backward(
-        factor, cot, branch, wo_spatial, comb, probs, tok, att, table, slab_shape
+        factor, cot, branch, wo_spatial, saved, tok, table, slab_shape
     )
     half_s = first_stages(own, send)
     token_grad = token_gradient(tok, wqkv_spatial, dcomb, stream_grad)

time: 141 us -> 137 us (0.972)
  Pallas kernels: 36.5 us -> 29.4 us
  local copies, waits for them, and re-layouts: 2.17 us -> 6.87 us
  blocking collectives: 58.6 us -> 55.6 us
  other arithmetic: 1.61 us -> 3.64 us
    ppermute x8, waiting for transfers between devices: 21.9 us -> 7.59 us  [shift(): return lax.ppermute(array, 'seq', pairs)]
    all_to_all x1, waiting for transfers between devices: 1.8 us -> 14.2 us  [trade(): return lax.all_to_all(array, 'seq', split_axis=0, concat_axis=0, tiled=True)]
    pallas_call x5, Pallas kernels: 36.5 us -> 29.4 us  [call(): pl.pallas_call(kernel, out_shape=tuple((jax.ShapeDtypeStruct(shape, B16)...]
    unnamed x4 -> x22, local copies, waits for them, and re-layouts: 0.76 us -> 3.91 us
    all_to_all x1, blocking collectives: 18.5 us -> 15.4 us  [last_stages(): lax.all_to_all(flat, 'seq', split_axis=0, concat_axis=0, tiled=True, axis...]
    squeeze x2, local copies, waits for them, and re-layouts: 0.11 us -> 1.66 us  [stage(): lax.dynamic_index_in_dim(chunks, (here + step) % size, 0, keepdims=False)]
  transfers between devices with their start and end apart: 10 -> 10, of which waited for: 8 -> 5; matrix products, arithmetic and copies ran while one was open for 0% -> 3% of each run, Pallas kernels for 3% -> 11%
where the time goes in v1:
time: 137 us; the launch traced here: 136 us
  blocking collectives  55.6 us (41%)
  Pallas kernels  29.4 us (21%)
  waiting for transfers between devices  22.4 us (16%)
  starting transfers between devices  17.4 us (13%)
  local copies, waits for them, and re-layouts  6.87 us (5%)
  other arithmetic  3.64 us (3%)
    all_to_all x1, blocking collectives, trade(): return lax.all_to_all(array, 'seq', split_axis=0, concat_axis=0, tiled=True)  40.2 us
    pallas_call x5, Pallas kernels, call(): pl.pallas_call(kernel, out_shape=tuple((jax.ShapeDtypeStruct(shape, B16)...  29.4 us
    all_to_all x1, blocking collectives, last_stages(): lax.all_to_all(flat, 'seq', split_axis=0, concat_axis=0, tiled=True, axis...  15.4 us
    all_to_all x1, waiting for transfers between devices, trade(): return lax.all_to_all(array, 'seq', split_axis=0, concat_axis=0, tiled=True)  14.2 us
    ppermute x8, starting transfers between devices, shift(): return lax.ppermute(array, 'seq', pairs)  8.88 us
    ppermute x8, waiting for transfers between devices, shift(): return lax.ppermute(array, 'seq', pairs)  7.59 us
    all_to_all x1, starting transfers between devices, trade(): return lax.all_to_all(array, 'seq', split_axis=0, concat_axis=0, tiled=True)  7.04 us
    unnamed x22, local copies, waits for them, and re-layouts  3.91 us
  transfers between devices with their start and end apart: 10, of which 5 were waited for; matrix products, arithmetic and copies ran while one was open for 3% of the time, Pallas kernels for 11%

profile of v1, /device:TPU:8, one launch (start us, length us, event | category | flops | bytes accessed | tf_op | source)
XLA Modules:
  0.0 136.1 jit_solution(18072469220024676393)
XLA Ops:
  0.6 7.2 %shard_map.110 = (bf16[128,8,384]{2,1,0:T(8,128)(2,1)}, bf16[9,512,512]{2,1,0:T(8,128)(2,1)}) custom-call(bf16[512,384]{1,0:T(8,128)(2,1)} %bitcast.36, bf16[512,384]{1,0:T(8,128)(2,1)} %bitcast.39, bf16[384,1152]{1,0:T(8,128)(2,1)} %w_ref.3, bf16[384,384]{1,0:T(8,128)(2,1)} %wo_ref.3), custom_call_target="tpu_custom_call" | custom-call | flops 2000000000 | bytes 1966080 | tf_op jit(solution)/shard_map/pallas_call | solution.py:73
  7.9 40.2 %all_to_all.15.slab_ref = bf16[128,8,384]{2,1,0:T(8,128)(2,1)S(1)} all-to-all(bf16[128,8,384]{2,1,0:T(8,128)(2,1)} %get-tuple-element.17), channel_id=1, replica_groups=mesh['dp'=2,'seq'=128] {'seq'}, dimensions={0} | all-to-all | bytes 1572864 | tf_op jit(solution)/shard_map/all_to_all | solution.py:421
  48.1 7.4 %shard_map.111 = (bf16[128,4,384]{2,1,0:T(4,128)(2,1)}, bf16[512,384]{1,0:T(8,128)(2,1)S(1)}, bf16[384,384]{1,0:T(8,128)(2,1)S(1)}, bf16[1152,512]{1,0:T(8,128)(2,1)S(1)}) custom-call(bf16[128,8,384]{2,1,0:T(8,128)(2,1)S(1)} %all_to_all.15.slab_ref, bf16[384,1152]{1,0:T(8,128)(2,1)S(1)} %copy-done.2, bf16[384,384]{1,0:T(8,128)(2,1)S(1)} %copy-done.4), custom_call_target="tpu_custom_call" | custom-call | flops 3000000000 | bytes 1966080 | tf_op jit(solution)/shard_map/pallas_call | solution.py:73
  55.5 7.0 %all-to-all-start.1 = ((bf16[128,4,384]{2,1,0:T(4,128)(2,1)}), bf16[128,4,384]{2,1,0:T(4,128)(2,1)S(1)}, u32[]{:S(2)}, u32[]{:S(2)}) async-start(bf16[128,4,384]{2,1,0:T(4,128)(2,1)} %get-tuple-element.18), calls=%async_computation.1 | async-start | bytes 786432 | tf_op jit(solution)/shard_map/all_to_all | solution.py:421
  62.6 1.0 copy-done.9
  63.6 2.6 %shard_map.114 = (bf16[4,8,24,384]{3,2,1,0:T(8,128)(2,1)S(1)}, bf16[4,8,24,384]{3,2,1,0:T(8,128)(2,1)}) custom-call(bf16[512,384]{1,0:T(8,128)(2,1)S(1)} %get-tuple-element.24.normed_ref, bf16[384,384]{1,0:T(8,128)(2,1)S(1)} %copy-done.9, bf16[1152,512]{1,0:T(8,128)(2,1)S(1)} %get-tuple-element.26.dct_ref, bf16[384,384]{1,0:T(8,128)(2,1)S(1)} %copy-done.6), custom_call_target="tpu_custom_call" | custom-call | flops 1500000000 | bytes 2162688 | tf_op jit(solution)/shard_map/pallas_call | solution.py:73
  66.5 14.2 %all-to-all-done.1.br_ref = bf16[128,4,384]{2,1,0:T(4,128)(2,1)S(1)} async-done(((bf16[128,4,384]{2,1,0:T(4,128)(2,1)}), bf16[128,4,384]{2,1,0:T(4,128)(2,1)S(1)}, u32[]{:S(2)}, u32[]{:S(2)}) %all-to-all-start.1) | async-done | bytes 393248 | tf_op jit(solution)/shard_map/all_to_all | solution.py:421
  80.7 1.0 copy-done.3
  81.7 1.0 copy-done.5
  82.7 1.0 copy-done.7
  83.6 10.3 %shard_map.112 = (bf16[4,8,24,384]{3,2,1,0:T(8,128)(2,1)S(1)}, bf16[4,8,24,384]{3,2,1,0:T(8,128)(2,1)}, bf16[512,384]{1,0:T(8,128)(2,1)S(1)}, bf16[512,1152]{1,0:T(8,128)(2,1)S(1)}) custom-call(bf16[512,384]{1,0:T(8,128)(2,1)S(1)} %bitcast.40, bf16[128,4,384]{2,1,0:T(4,128)(2,1)S(1)} %all-to-all-done.1.br_ref, bf16[384,384]{1,0:T(8,128)(2,1)S(1)} %copy-done.5, ...), custom_call_target="tpu_custom_call" | custom-call | flops 4000000000 | bytes 6488064 | tf_op jit(solution)/shard_map/pallas_call | solution.py:73
  94.3 1.2 add_convert_fusion
  96.4 0.9 collective-permute-start.7
  97.3 1.9 %collective-permute-start.6 = (bf16[8,24,384]{2,1,0:T(8,128)(2,1)}, bf16[8,24,384]{2,1,0:T(8,128)(2,1)S(1)}, u32[]{:S(2)}, u32[]{:S(2)}) collective-permute-start(bf16[8,24,384]{2,1,0:T(8,128)(2,1)} %get-tuple-element.34), channel_id=1, source_target_pairs={{0,64},{1,65},{2,66},{3,67},{4,68},{5,69},{6,70},{7,71},{8,72},{9,... | collective-permute-start | bytes 442376 | tf_op jit(solution)/shard_map/ppermute | solution.py:353
  99.2 1.2 add_convert_fusion.1
  101.2 3.2 %collective-permute-start.3 = (bf16[8,24,384]{2,1,0:T(8,128)(2,1)}, bf16[8,24,384]{2,1,0:T(8,128)(2,1)S(1)}, u32[]{:S(2)}, u32[]{:S(2)}) collective-permute-start(bf16[8,24,384]{2,1,0:T(8,128)(2,1)} %get-tuple-element.30), channel_id=1, source_target_pairs={{0,96},{1,97},{2,98},{3,99},{4,100},{5,101},{6,102},{7,103},{8,104... | collective-permute-start | bytes 442376 | tf_op jit(solution)/shard_map/ppermute | solution.py:353
  104.8 1.8 %collective-permute-start.1 = (bf16[8,24,384]{2,1,0:T(8,128)(2,1)S(1)}, bf16[8,24,384]{2,1,0:T(8,128)(2,1)S(1)}, u32[]{:S(2)}, u32[]{:S(2)}) collective-permute-start(bf16[8,24,384]{2,1,0:T(8,128)(2,1)S(1)} %get-tuple-element.29), channel_id=1, source_target_pairs={{0,32},{1,33},{2,34},{3,35},{4,36},{5,37},{6,38},{7,39},{8,40},{9,... | collective-permute-start | bytes 442376 | tf_op jit(solution)/shard_map/ppermute | solution.py:353
  106.7 3.1 %collective-permute-done.5 = bf16[8,24,384]{2,1,0:T(8,128)(2,1)} collective-permute-done((bf16[8,24,384]{2,1,0:T(8,128)(2,1)}, bf16[8,24,384]{2,1,0:T(8,128)(2,1)}, u32[]{:S(2)}, u32[]{:S(2)}) %collective-permute-start.5) | collective-permute-done | bytes 147488 | tf_op jit(solution)/shard_map/ppermute | solution.py:353
  109.8 2.9 %collective-permute-done.2 = bf16[8,24,384]{2,1,0:T(8,128)(2,1)S(1)} collective-permute-done((bf16[8,24,384]{2,1,0:T(8,128)(2,1)}, bf16[8,24,384]{2,1,0:T(8,128)(2,1)S(1)}, u32[]{:S(2)}, u32[]{:S(2)}) %collective-permute-start.2) | collective-permute-done | bytes 147488 | tf_op jit(solution)/shard_map/ppermute | solution.py:353
  112.7 1.5 %collective-permute-done.1 = bf16[8,24,384]{2,1,0:T(8,128)(2,1)S(1)} collective-permute-done((bf16[8,24,384]{2,1,0:T(8,128)(2,1)S(1)}, bf16[8,24,384]{2,1,0:T(8,128)(2,1)S(1)}, u32[]{:S(2)}, u32[]{:S(2)}) %collective-permute-start.1) | collective-permute-done | bytes 147488 | tf_op jit(solution)/shard_map/ppermute | solution.py:353
  114.2 1.1 fusion.2
  115.5 15.4 %all_to_all.16 = bf16[16,24,384]{2,1,0:T(8,128)(2,1)S(1)} all-to-all(bf16[16,24,384]{2,1,0:T(8,128)(2,1)S(1)} %bitcast.41), channel_id=1, replica_groups={{0,2,4,6,8,10,12,14,16,18,20,22,24,26,28,30},{1,3,5,7,9,11,13,15,17,19,..., dimensions={0} | all-to-all | bytes 589824 | tf_op jit(solution)/shard_map/all_to_all | solution.py:404
  131.0 1.4 %collective-permute-start.8 = (bf16[24,384]{1,0:T(8,128)(2,1)S(1)}, bf16[24,384]{1,0:T(8,128)(2,1)S(1)}, u32[]{:S(2)}, u32[]{:S(2)}) collective-permute-start(bf16[24,384]{1,0:T(8,128)(2,1)S(1)} %reduce_sum.12), channel_id=1, source_target_pairs={{0,128},{128,0},{1,129},{129,1},{2,130},{130,2},{3,131},{131,3},{4... | collective-permute-start | bytes 55304 | tf_op jit(solution)/shard_map/ppermute | solution.py:408
  132.4 1.8 %shard_map.113 = bf16[512,384]{1,0:T(8,128)(2,1)} custom-call(bf16[512,384]{1,0:T(8,128)(2,1)S(1)} %bitcast.38, bf16[384,1152]{1,0:T(8,128)(2,1)S(1)} %copy-done, bf16[512,1152]{1,0:T(8,128)(2,1)S(1)} %get-tuple-element.20.dcomb_ref, bf16[512,384]{1,0:T(8,128)(2,1)S(1)} %get-tuple-element.21.sg_ref), custom_call_target="tpu_custom_call" | custom-call | flops 500000000 | bytes 2850816 | tf_op jit(solution)/shard_map/pallas_call | solution.py:73
  (38 shorter events, 4.7 us)
Async XLA Ops:
  7.8 40.2 %copy-start.2 = (bf16[384,1152]{1,0:T(8,128)(2,1)S(1)}, bf16[384,1152]{1,0:T(8,128)(2,1)}, u32[]{:S(2)}) copy-start(bf16[384,1152]{1,0:T(8,128)(2,1)} %w_ref.2) | copy-start | bytes 2654212
  7.9 40.2 %copy-start.4 = (bf16[384,384]{1,0:T(8,128)(2,1)S(1)}, bf16[384,384]{1,0:T(8,128)(2,1)}, u32[]{:S(2)}) copy-start(bf16[384,384]{1,0:T(8,128)(2,1)} %wo_ref.2) | copy-start | bytes 884740
  48.1 14.5 %copy-start.6 = (bf16[384,384]{1,0:T(8,128)(2,1)S(1)}, bf16[384,384]{1,0:T(8,128)(2,1)}, u32[]{:S(2)}) copy-start(bf16[384,384]{1,0:T(8,128)(2,1)} %constant.81.clone.onehot_ref) | copy-start | bytes 884740
  55.5 7.1 %copy-start.8 = (bf16[384,384]{1,0:T(8,128)(2,1)}, bf16[384,384]{1,0:T(8,128)(2,1)S(1)}, u32[]{:S(2)}) copy-start(bf16[384,384]{1,0:T(8,128)(2,1)S(1)} %get-tuple-element.25.go_ref) | copy-start | bytes 884740
  55.5 25.2 %all-to-all-start.1 = ((bf16[128,4,384]{2,1,0:T(4,128)(2,1)}), bf16[128,4,384]{2,1,0:T(4,128)(2,1)S(1)}, u32[]{:S(2)}, u32[]{:S(2)}) async-start(bf16[128,4,384]{2,1,0:T(4,128)(2,1)} %get-tuple-element.18), calls=%async_computation.1 | async-start | bytes 786432 | tf_op jit(solution)/shard_map/all_to_all | solution.py:421
  62.6 1.0 copy-start.9
  63.6 17.2 %copy-start.1 = (bf16[1,1,512,384]{3,2,1,0:T(8,128)(2,1)S(1)}, bf16[1,1,512,384]{3,2,1,0:T(8,128)(2,1)}, u32[]{:S(2)}) copy-start(bf16[1,1,512,384]{3,2,1,0:T(8,128)(2,1)} %param.7) | copy-start | bytes 1179652
  66.2 28.1 %collective-permute-start.4 = (bf16[4,8,24,384]{3,2,1,0:T(8,128)(2,1)}, bf16[4,8,24,384]{3,2,1,0:T(8,128)(2,1)}, u32[]{:S(2)}, u32[]{:S(2)}) collective-permute-start(bf16[4,8,24,384]{3,2,1,0:T(8,128)(2,1)} %get-tuple-element.28), channel_id=1, source_target_pairs={{0,1},{1,0},{2,3},{3,2},{4,5},{5,4},{6,7},{7,6},{8,9},{9,8},{10,11... | collective-permute-start | bytes 1769480 | tf_op jit(solution)/shard_map/ppermute | solution.py:353
  80.7 1.0 copy-start.3
  81.7 1.0 copy-start.5
  82.7 1.0 copy-start.7
  94.0 5.2 %collective-permute-start = (bf16[4,8,24,384]{3,2,1,0:T(8,128)(2,1)}, bf16[4,8,24,384]{3,2,1,0:T(8,128)(2,1)}, u32[]{:S(2)}, u32[]{:S(2)}) collective-permute-start(bf16[4,8,24,384]{3,2,1,0:T(8,128)(2,1)} %get-tuple-element.23), channel_id=1, source_target_pairs={{0,1},{1,0},{2,3},{3,2},{4,5},{5,4},{6,7},{7,6},{8,9},{9,8},{10,11... | collective-permute-start | bytes 1769480 | tf_op jit(solution)/shard_map/ppermute | solution.py:353
  95.5 4.9 %copy-start.10 = (bf16[4,8,24,384]{3,2,1,0:T(8,128)(2,1)}, bf16[4,8,24,384]{3,2,1,0:T(8,128)(2,1)S(1)}, u32[]{:S(2)}) copy-start(bf16[4,8,24,384]{3,2,1,0:T(8,128)(2,1)S(1)} %add_convert_fusion) | copy-start | bytes 1769476
  96.4 8.5 %collective-permute-start.7 = (bf16[8,24,384]{2,1,0:T(8,128)(2,1)S(1)}, bf16[8,24,384]{2,1,0:T(8,128)(2,1)S(1)}, u32[]{:S(2)}, u32[]{:S(2)}) collective-permute-start(bf16[8,24,384]{2,1,0:T(8,128)(2,1)S(1)} %get-tuple-element.33), channel_id=1, source_target_pairs={{0,96},{1,97},{2,98},{3,99},{4,100},{5,101},{6,102},{7,103},{8,104... | collective-permute-start | bytes 442376 | tf_op jit(solution)/shard_map/ppermute | solution.py:353
  97.3 9.4 %collective-permute-start.6 = (bf16[8,24,384]{2,1,0:T(8,128)(2,1)}, bf16[8,24,384]{2,1,0:T(8,128)(2,1)S(1)}, u32[]{:S(2)}, u32[]{:S(2)}) collective-permute-start(bf16[8,24,384]{2,1,0:T(8,128)(2,1)} %get-tuple-element.34), channel_id=1, source_target_pairs={{0,64},{1,65},{2,66},{3,67},{4,68},{5,69},{6,70},{7,71},{8,72},{9,... | collective-permute-start | bytes 442376 | tf_op jit(solution)/shard_map/ppermute | solution.py:353
  99.2 10.6 %collective-permute-start.5 = (bf16[8,24,384]{2,1,0:T(8,128)(2,1)}, bf16[8,24,384]{2,1,0:T(8,128)(2,1)}, u32[]{:S(2)}, u32[]{:S(2)}) collective-permute-start(bf16[8,24,384]{2,1,0:T(8,128)(2,1)} %get-tuple-element.32), channel_id=1, source_target_pairs={{0,32},{1,33},{2,34},{3,35},{4,36},{5,37},{6,38},{7,39},{8,40},{9,... | collective-permute-start | bytes 442376 | tf_op jit(solution)/shard_map/ppermute | solution.py:353
  101.2 8.6 %collective-permute-start.3 = (bf16[8,24,384]{2,1,0:T(8,128)(2,1)}, bf16[8,24,384]{2,1,0:T(8,128)(2,1)S(1)}, u32[]{:S(2)}, u32[]{:S(2)}) collective-permute-start(bf16[8,24,384]{2,1,0:T(8,128)(2,1)} %get-tuple-element.30), channel_id=1, source_target_pairs={{0,96},{1,97},{2,98},{3,99},{4,100},{5,101},{6,102},{7,103},{8,104... | collective-permute-start | bytes 442376 | tf_op jit(solution)/shard_map/ppermute | solution.py:353
  104.4 8.3 %collective-permute-start.2 = (bf16[8,24,384]{2,1,0:T(8,128)(2,1)}, bf16[8,24,384]{2,1,0:T(8,128)(2,1)S(1)}, u32[]{:S(2)}, u32[]{:S(2)}) collective-permute-start(bf16[8,24,384]{2,1,0:T(8,128)(2,1)} %get-tuple-element.31), channel_id=1, source_target_pairs={{0,64},{1,65},{2,66},{3,67},{4,68},{5,69},{6,70},{7,71},{8,72},{9,... | collective-permute-start | bytes 442376 | tf_op jit(solution)/shard_map/ppermute | solution.py:353
  104.8 9.4 %collective-permute-start.1 = (bf16[8,24,384]{2,1,0:T(8,128)(2,1)S(1)}, bf16[8,24,384]{2,1,0:T(8,128)(2,1)S(1)}, u32[]{:S(2)}, u32[]{:S(2)}) collective-permute-start(bf16[8,24,384]{2,1,0:T(8,128)(2,1)S(1)} %get-tuple-element.29), channel_id=1, source_target_pairs={{0,32},{1,33},{2,34},{3,35},{4,36},{5,37},{6,38},{7,39},{8,40},{9,... | collective-permute-start | bytes 442376 | tf_op jit(solution)/shard_map/ppermute | solution.py:353
  115.4 17.0 %copy-start = (bf16[384,1152]{1,0:T(8,128)(2,1)S(1)}, bf16[384,1152]{1,0:T(8,128)(2,1)}, u32[]{:S(2)}) copy-start(bf16[384,1152]{1,0:T(8,128)(2,1)} %w_ref.3) | copy-start | bytes 2654212
  131.0 3.8 %collective-permute-start.8 = (bf16[24,384]{1,0:T(8,128)(2,1)S(1)}, bf16[24,384]{1,0:T(8,128)(2,1)S(1)}, u32[]{:S(2)}, u32[]{:S(2)}) collective-permute-start(bf16[24,384]{1,0:T(8,128)(2,1)S(1)} %reduce_sum.12), channel_id=1, source_target_pairs={{0,128},{128,0},{1,129},{129,1},{2,130},{130,2},{3,131},{131,3},{4... | collective-permute-start | bytes 55304 | tf_op jit(solution)/shard_map/ppermute | solution.py:408

commit v2 on v1

--- a/solution.py
+++ b/solution.py
@@ -2,7 +2,6 @@
 
 import jax
 import jax.numpy as jnp
-import numpy as np
 from jax import lax
 from jax.experimental import pallas as pl
 from jax.experimental.pallas import tpu as pltpu
@@ -138,8 +137,9 @@
     wo_in.wait()
     out = (x + mm(att, wo_ref[...])).astype(B16)
     cot_in.wait()
-    half = (slab_ref.shape[0], slab_ref.shape[1] // 2, width)
-    slab_ref[...] = jnp.concatenate([out.reshape(half), cot_ref[...].reshape(half)], 1)
+    half = (slab_ref.shape[0],) + slab_ref.shape[2:]
+    slab_ref[:, 0] = out.reshape(half)
+    slab_ref[:, 1] = cot_ref[...].reshape(half)
     for copy in outs:
         copy.wait()
 
@@ -156,16 +156,14 @@
 
 
 def temporal_kernel(
-    factor, slab_ref, w_ref, wo_ref, branch_ref, normed_ref, go_ref, dct_ref, _,
+    factor, slab_ref, w_ref, wo_ref, branch_ref, normed_ref, go_ref, dct_ref, sems,
 ):
-    frames, both, width = slab_ref.shape
-    patches = both // 2
+    frames, _, patches, width = slab_ref.shape
     rows = frames * patches
     hw = width // HEADS
     gather = regroup(rows, frames, patches)
-    slab = slab_ref[...]
-    x = mm(gather, slab[:, :patches].reshape(rows, width))
-    cot = mm(gather, slab[:, patches:].reshape(rows, width)).astype(B16)
+    x = mm(gather, slab_ref[:, 0].reshape(rows, width))
+    cot = mm(gather, slab_ref[:, 1].reshape(rows, width)).astype(B16)
     scaled, inverse = normalize(x)
     normed = scaled.astype(B16)
     normed_ref[...] = normed
@@ -214,19 +212,37 @@
 
 
 def temporal(factor, slab, w, wo):
-    frames, both, width = slab.shape
-    rows = frames * both // 2
+    frames, _, patches, width = slab.shape
+    rows = frames * patches
     return call(
         functools.partial(temporal_kernel, factor), (slab, w, wo),
-        ((frames, both // 2, width), (rows, width), wo.shape, (3 * width, rows)),
+        ((frames, patches, width), (rows, width), wo.shape, (3 * width, rows)),
         [VM] * 3, [VM] * 4, [], 1, 3_000_000_000, 400_000, 48,
     )
 
 
-def spread(onehot, gq, go, slab_ref, own_ref, send_ref):
+def exchange_order(cores, depth, rows, a, b):
+    each = a + b
+    pair = rows // each
+    row = lax.broadcasted_iota(jnp.int32, (cores * depth * rows, 1), 0)
+    slab = lax.shift_right_logical(row * ((1 << 16) // each + 1), 16)
+    i = row - slab * each
+    yh = slab & (pair - 1)
+    z = lax.shift_right_logical(slab, pair.bit_length() - 1) & (depth - 1)
+    core = lax.shift_right_logical(slab, (pair * depth).bit_length() - 1)
+    member = (yh * depth + z) * cores + core
+    source = jnp.where(i < a, member * a + i, cores * depth * pair * a + member * b + i - a)
+    column = lax.broadcasted_iota(jnp.int32, (row.shape[0], row.shape[0]), 1)
+    return (column == source).astype(F32).astype(B16)
+
+
+def spread(gq, go, slab_ref, own_ref, send_ref):
     here = lax.axis_index("seq") % slab_ref.shape[0]
     groups = slab_ref.shape[1]
     a, b = gq.shape[0] // groups, go.shape[0] // groups
+    cores, _, depth, rows, _ = slab_ref.shape
+    each = a // (cores * depth * 2), b // (cores * depth * 2)
+    onehot = exchange_order(cores, depth, rows, *each)
     for x in range(groups):
         source = jnp.concatenate([gq[x * a : (x + 1) * a], go[x * b : (x + 1) * b]], 0)
         moved = mm(onehot, source).astype(B16)
@@ -235,20 +251,20 @@
         own_ref[x] = slab_ref[here, x]
 
 
-def weight_kernel(factor, normed_ref, go_ref, dct_ref, onehot_ref, own_ref, send_ref, slab_ref, _):
+def weight_kernel(factor, normed_ref, go_ref, dct_ref, own_ref, send_ref, slab_ref, _):
     gq = (mm(dct_ref[...], normed_ref[...]) * factor).astype(B16)
-    spread(onehot_ref[...], gq, go_ref[...], slab_ref, own_ref, send_ref)
-
-
-def weight_slabs(factor, normed, go, dct, onehot, shape):
-    return call(
-        functools.partial(weight_kernel, factor), (normed, go, dct, onehot),
-        (shape[1:], shape[1:]), [VM] * 4, [VM] * 2, [shape], 1, 1_500_000_000, 0, 48,
+    spread(gq, go_ref[...], slab_ref, own_ref, send_ref)
+
+
+def weight_slabs(factor, normed, go, dct, shape):
+    return call(
+        functools.partial(weight_kernel, factor), (normed, go, dct),
+        (shape[1:], shape[1:]), [VM] * 3, [VM] * 2, [shape], 1, 1_500_000_000, 0, 48,
     )
 
 
 def spatial_backward_kernel(
-    factor, ct_ref, br_ref, wo_ref, saved_hbm, tok_ref, onehot_ref,
+    factor, ct_ref, br_ref, wo_ref, saved_hbm, tok_ref,
     own_ref, send_ref, sg_ref, dcomb_ref,
     comb_ref, probs_ref, slab_ref, sems,
 ):
@@ -267,7 +283,7 @@
     gt = g.T
     scaled, _ = normalize(tok_ref[...].astype(F32))
     normed = scaled.astype(B16)
-    for copy in comb_in:
+    for copy in comb_in + probs_in:
         copy.wait()
     q = comb_ref[:, :width] * (hw ** -0.5)
     kt = comb_ref[:, width : 2 * width].T
@@ -278,7 +294,6 @@
         dk = dv = 0.0
         for sub in range(2):
             head = 2 * pair + sub
-            probs_in[head].wait()
             p = probs_ref[head]
             ds = score_back(p, mm(values, one_head(gt[lanes], sub, hw, 0)))
             dqt = mm(kt[head * hw : (head + 1) * hw], ds) * (hw ** -0.5)
@@ -293,20 +308,20 @@
     dct = jnp.concatenate([dqt, dk.T, dv.T], 0)
     gq = (mm(dct, normed) * factor).astype(B16)
     go = (mm(sg.T, comb_ref[:, 3 * width :]) * factor).astype(B16)
-    spread(onehot_ref[...], gq, go, slab_ref, own_ref, send_ref)
+    spread(gq, go, slab_ref, own_ref, send_ref)
     dcomb_ref[:, :width] = dqt.T
     dcomb_ref[:, width : 2 * width] = dk
     dcomb_ref[:, 2 * width :] = dv
 
 
-def spatial_backward(factor, ct, branch, wo, saved, tokens, onehot, shape):
+def spatial_backward(factor, ct, branch, wo, saved, tokens, shape):
     rows, width = tokens.shape
-    arrays = (ct, branch, wo, saved, tokens, onehot)
+    arrays = (ct, branch, wo, saved, tokens)
     square, wide = (rows, width), (rows, 3 * width)
     return call(
         functools.partial(spatial_backward_kernel, factor), arrays,
         (shape[1:], shape[1:], square, wide),
-        [VM, VM, VM, HBM, VM, VM], [VM] * 4,
+        [VM, VM, VM, HBM, VM], [VM] * 4,
         [(rows, 4 * width), (HEADS, rows, rows), shape], 3 + HEADS, 4_000_000_000, 0, 48,
     )
 
@@ -353,37 +368,55 @@
     return lax.ppermute(array, "seq", pairs)
 
 
-def stage(chunks, name):
-    size = chunks.shape[0]
-    here = coordinate(name)
-    total = lax.dynamic_index_in_dim(chunks, here, 0, keepdims=False).astype(F32)
-    for step in range(1, size):
-        part = lax.dynamic_index_in_dim(chunks, (here + step) % size, 0, keepdims=False)
-        total = total + shift(part, name, step).astype(F32)
-    return total
-
-
-def slab_order(width):
+def slab_shape(width):
     sizes = dict(SEQ)
-    a, b = 3 * width // seq_size(), width // seq_size()
-    group = seq_size() // sizes["x"]
-    table = np.zeros(((a + b) * group, (a + b) * group), np.float32)
-    row = 0
-    for core in range(sizes["core"]):
-        for z in range(sizes["z"]):
-            for yh in range(sizes["yh"]):
-                member = (yh * sizes["z"] + z) * sizes["core"] + core
-                for i in range(a + b):
-                    source = member * a + i if i < a else group * a + member * b + i - a
-                    table[row, source] = 1.0
-                    row += 1
-    shape = (sizes["core"], sizes["x"], sizes["z"], sizes["yh"] * (a + b), width)
-    return jnp.asarray(table, B16), shape
+    rows = sizes["yh"] * 4 * width // seq_size()
+    return (sizes["core"], sizes["x"], sizes["z"], rows, width)
+
+
+def total_of(refs):
+    here = coordinate("x")
+    total = refs[0][here].astype(F32)
+    for ref in refs[1:]:
+        total = total + ref[...].astype(F32)
+    return total.astype(B16)
+
+
+def sum_kernel(*refs):
+    refs[-2][...] = total_of(refs[:-2])
+
+
+def join_kernel(early_ref, *refs):
+    out_ref = refs[-2]
+    late, early = total_of(refs[:-2]), early_ref[...]
+    pair, rows = out_ref.shape[0], out_ref.shape[2] // 2
+    for yh in range(pair):
+        part = slice(yh * rows, (yh + 1) * rows)
+        out_ref[yh] = jnp.concatenate([late[:, part], early[:, part]], 1)
 
 
 def first_stages(own, send):
     part = (own.astype(F32) + shift(send, "core", 1).astype(F32)).astype(B16)
-    return stage(part, "x").astype(B16)
+    here, size = coordinate("x"), part.shape[0]
+    return (part,) + tuple(
+        shift(lax.dynamic_index_in_dim(part, (here + k) % size, 0, keepdims=False), "x", k)
+        for k in range(1, size)
+    )
+
+
+def sum_early(parts):
+    return call(
+        sum_kernel, parts, (parts[0].shape[1:],), [VM] * len(parts), [VM], [],
+        1, 1_000_000, 0, 48,
+    )[0]
+
+
+def join(early, parts):
+    z, rows, width = early.shape
+    return call(
+        join_kernel, (early, *parts), ((2, z, rows, width),), [VM] * (1 + len(parts)),
+        [VM], [], 1, 1_000_000, 0, 48,
+    )[0]
 
 
 def groups_of(*names):
@@ -412,10 +445,10 @@
 def on_device(tokens, cotangent, wqkv_spatial, wo_spatial, wqkv_temporal, wo_temporal):
     clips, frames, patches, width = tokens.shape
     factor = (clips * frames * patches * lax.axis_size("dp") * seq_size()) ** (-0.5)
-    table, slab_shape = slab_order(width)
+    shape = slab_shape(width)
     tok = tokens.reshape(patches, width)
     cot = cotangent.reshape(patches, width)
-    traded = (seq_size(), 2 * patches // seq_size(), width)
+    traded = (seq_size(), 2, patches // seq_size(), width)
 
     def trade(array):
         return lax.all_to_all(array, "seq", split_axis=0, concat_axis=0, tiled=True)
@@ -423,21 +456,15 @@
     stream, saved = spatial_forward(tok, cot, wqkv_spatial, wo_spatial, traded)
     branch, normed_t, go_t, dct = temporal(factor, trade(stream), wqkv_temporal, wo_temporal)
     branch = trade(branch)
-    own, send = weight_slabs(factor, normed_t, go_t, dct, table, slab_shape)
+    own, send = weight_slabs(factor, normed_t, go_t, dct, shape)
     half_t = first_stages(own, send)
     own, send, stream_grad, dcomb = spatial_backward(
-        factor, cot, branch, wo_spatial, saved, tok, table, slab_shape
+        factor, cot, branch, wo_spatial, saved, tok, shape
     )
     half_s = first_stages(own, send)
     token_grad = token_gradient(tok, wqkv_spatial, dcomb, stream_grad)
-    z, rows = half_s.shape[:2]
-    joined = jnp.concatenate(
-        [
-            jnp.moveaxis(half.reshape(z, 2, rows // 2, width), 1, 0)
-            for half in (half_s, half_t)
-        ],
-        2,
-    )
+    half_t = sum_early(half_t)
+    joined = join(half_t, half_s)
     own = last_stages(joined)
     a, b = 3 * width // seq_size(), width // seq_size()
     shares = (own[:a].T, own[a : a + b].T, own[a + b : 2 * a + b].T, own[2 * a + b :].T)

time: 137 us -> 133 us (0.971); the launches traced: 136 us -> 131 us
  local copies, waits for them, and re-layouts: 6.87 us -> 3.32 us
  waiting for transfers between devices: 22.4 us -> 25.2 us
  starting transfers between devices: 17.4 us -> 15.7 us
    ppermute x8, waiting for transfers between devices: 7.59 us -> 9.58 us  [shift(): return lax.ppermute(array, 'seq', pairs)]
    unnamed x22 -> x12, local copies, waits for them, and re-layouts: 3.91 us -> 1.98 us
    ppermute x8, starting transfers between devices: 8.88 us -> 7.11 us  [shift(): return lax.ppermute(array, 'seq', pairs)]
    squeeze x2, local copies, waits for them, and re-layouts: 1.66 us -> 0.11 us  [first_stages(): lax.dynamic_index_in_dim(part, (here + k) % size, 0, keepdims=False)]
    pallas_call x5 -> x7, Pallas kernels: 29.4 us -> 28.7 us  [call(): pl.pallas_call(kernel, out_shape=tuple((jax.ShapeDtypeStruct(shape, B16)...]
  transfers between devices with their start and end apart: 10 -> 10, of which waited for: 5 -> 6; matrix products, arithmetic and copies ran while one was open for 3% -> 2% of each run, Pallas kernels for 11% -> 11%
where the time goes in v2:
time: 133 us; the launch traced here: 131 us
  blocking collectives  54.5 us (41%)
  Pallas kernels  28.7 us (22%)
  waiting for transfers between devices  25.2 us (19%)
  starting transfers between devices  15.7 us (12%)
  local copies, waits for them, and re-layouts  3.32 us (2%)
  other arithmetic  2.47 us (2%)
    all_to_all x1, blocking collectives, trade(): return lax.all_to_all(array, 'seq', split_axis=0, concat_axis=0, tiled=True)  40.2 us
    pallas_call x7, Pallas kernels, call(): pl.pallas_call(kernel, out_shape=tuple((jax.ShapeDtypeStruct(shape, B16)...  28.7 us
    all_to_all x1, waiting for transfers between devices, trade(): return lax.all_to_all(array, 'seq', split_axis=0, concat_axis=0, tiled=True)  15.1 us
    all_to_all x1, blocking collectives, last_stages(): lax.all_to_all(flat, 'seq', split_axis=0, concat_axis=0, tiled=True, axis...  14.3 us
    ppermute x8, waiting for transfers between devices, shift(): return lax.ppermute(array, 'seq', pairs)  9.58 us
    ppermute x8, starting transfers between devices, shift(): return lax.ppermute(array, 'seq', pairs)  7.11 us
    all_to_all x1, starting transfers between devices, trade(): return lax.all_to_all(array, 'seq', split_axis=0, concat_axis=0, tiled=True)  7.05 us
  transfers between devices with their start and end apart: 10, of which 6 were waited for; matrix products, arithmetic and copies ran while one was open for 2% of the time, Pallas kernels for 11%

profile of v2, /device:TPU:8, one launch (start us, length us, event | category | flops | bytes accessed | tf_op | source)
XLA Modules:
  0.0 130.7 jit_solution(10391150936236832915)
XLA Ops:
  0.6 7.2 %shard_map.101 = (bf16[128,2,4,384]{3,2,1,0:T(4,128)(2,1)}, bf16[9,512,512]{2,1,0:T(8,128)(2,1)}) custom-call(bf16[512,384]{1,0:T(8,128)(2,1)} %bitcast.25, bf16[512,384]{1,0:T(8,128)(2,1)} %bitcast.28, bf16[384,1152]{1,0:T(8,128)(2,1)} %w_ref.3, bf16[384,384]{1,0:T(8,128)(2,1)} %wo_ref.3), custom_call_target="tpu_custom_call" | custom-call | flops 2000000000 | bytes 1966080 | tf_op jit(solution)/shard_map/pallas_call | solution.py:72
  7.8 40.2 %all_to_all.15.slab_ref = bf16[128,2,4,384]{3,2,1,0:T(4,128)(2,1)S(1)} all-to-all(bf16[128,2,4,384]{3,2,1,0:T(4,128)(2,1)} %get-tuple-element.17), channel_id=1, replica_groups=mesh['dp'=2,'seq'=128] {'seq'}, dimensions={0} | all-to-all | bytes 1572864 | tf_op jit(solution)/shard_map/all_to_all | solution.py:454
  48.0 7.4 %shard_map.102 = (bf16[128,4,384]{2,1,0:T(4,128)(2,1)}, bf16[512,384]{1,0:T(8,128)(2,1)S(1)}, bf16[384,384]{1,0:T(8,128)(2,1)S(1)}, bf16[1152,512]{1,0:T(8,128)(2,1)S(1)}) custom-call(bf16[128,2,4,384]{3,2,1,0:T(4,128)(2,1)S(1)} %all_to_all.15.slab_ref, bf16[384,1152]{1,0:T(8,128)(2,1)S(1)} %copy-done.2, bf16[384,384]{1,0:T(8,128)(2,1)S(1)} %copy-done.4), custom_call_target="tpu_custom_call" | custom-call | flops 3000000000 | bytes 1966080 | tf_op jit(solution)/shard_map/pallas_call | solution.py:72
  55.5 7.1 %all-to-all-start.1 = ((bf16[128,4,384]{2,1,0:T(4,128)(2,1)}), bf16[128,4,384]{2,1,0:T(4,128)(2,1)S(1)}, u32[]{:S(2)}, u32[]{:S(2)}) async-start(bf16[128,4,384]{2,1,0:T(4,128)(2,1)} %get-tuple-element.18), calls=%async_computation.1 | async-start | bytes 786432 | tf_op jit(solution)/shard_map/all_to_all | solution.py:454
  62.5 2.7 %shard_map.105 = (bf16[4,8,24,384]{3,2,1,0:T(8,128)(2,1)S(1)}, bf16[4,8,24,384]{3,2,1,0:T(8,128)(2,1)}) custom-call(bf16[512,384]{1,0:T(8,128)(2,1)S(1)} %get-tuple-element.22.normed_ref, bf16[384,384]{1,0:T(8,128)(2,1)S(1)} %get-tuple-element.23.go_ref, bf16[1152,512]{1,0:T(8,128)(2,1)S(1)} %get-tuple-element.24.dct_ref), custom_call_target="tpu_custom_call" | custom-call | flops 1500000000 | bytes 1867776 | tf_op jit(solution)/shard_map/pallas_call | solution.py:72
  65.6 15.1 %all-to-all-done.1.br_ref = bf16[128,4,384]{2,1,0:T(4,128)(2,1)S(1)} async-done(((bf16[128,4,384]{2,1,0:T(4,128)(2,1)}), bf16[128,4,384]{2,1,0:T(4,128)(2,1)S(1)}, u32[]{:S(2)}, u32[]{:S(2)}) %all-to-all-start.1) | async-done | bytes 393248 | tf_op jit(solution)/shard_map/all_to_all | solution.py:454
  80.7 1.0 copy-done.3
  81.7 1.0 copy-done.5
  82.6 9.4 %shard_map.103 = (bf16[4,8,24,384]{3,2,1,0:T(8,128)(2,1)S(1)}, bf16[4,8,24,384]{3,2,1,0:T(8,128)(2,1)}, bf16[512,384]{1,0:T(8,128)(2,1)S(1)}, bf16[512,1152]{1,0:T(8,128)(2,1)S(1)}) custom-call(bf16[512,384]{1,0:T(8,128)(2,1)S(1)} %bitcast.29, bf16[128,4,384]{2,1,0:T(4,128)(2,1)S(1)} %all-to-all-done.1.br_ref, bf16[384,384]{1,0:T(8,128)(2,1)S(1)} %copy-done.5, ...), custom_call_target="tpu_custom_call" | custom-call | flops 4000000000 | bytes 6193152 | tf_op jit(solution)/shard_map/pallas_call | solution.py:72
  92.3 1.2 add_convert_fusion.1.refs_0_
  93.6 0.9 collective-permute-start.1
  94.4 1.6 %collective-permute-start.2 = (bf16[8,24,384]{2,1,0:T(8,128)(2,1)S(1)}, bf16[8,24,384]{2,1,0:T(8,128)(2,1)S(1)}, u32[]{:S(2)}, u32[]{:S(2)}) collective-permute-start(bf16[8,24,384]{2,1,0:T(8,128)(2,1)S(1)} %get-tuple-element.33), channel_id=1, source_target_pairs={{0,64},{1,65},{2,66},{3,67},{4,68},{5,69},{6,70},{7,71},{8,72},{9,... | collective-permute-start | bytes 442376 | tf_op jit(solution)/shard_map/ppermute | solution.py:368
  96.1 1.1 collective-permute-start.3
  97.2 1.2 add_convert_fusion.refs_0_
  98.5 1.0 collective-permute-start.5
  99.5 1.9 %collective-permute-start.6 = (bf16[8,24,384]{2,1,0:T(8,128)(2,1)S(1)}, bf16[8,24,384]{2,1,0:T(8,128)(2,1)S(1)}, u32[]{:S(2)}, u32[]{:S(2)}) collective-permute-start(bf16[8,24,384]{2,1,0:T(8,128)(2,1)S(1)} %get-tuple-element.30), channel_id=1, source_target_pairs={{0,64},{1,65},{2,66},{3,67},{4,68},{5,69},{6,70},{7,71},{8,72},{9,... | collective-permute-start | bytes 442376 | tf_op jit(solution)/shard_map/ppermute | solution.py:368
  101.4 3.4 %collective-permute-done.1.refs_1_ = bf16[8,24,384]{2,1,0:T(8,128)(2,1)S(1)} collective-permute-done((bf16[8,24,384]{2,1,0:T(8,128)(2,1)S(1)}, bf16[8,24,384]{2,1,0:T(8,128)(2,1)S(1)}, u32[]{:S(2)}, u32[]{:S(2)}) %collective-permute-start.1) | collective-permute-done | bytes 147488 | tf_op jit(solution)/shard_map/ppermute | solution.py:368
  104.8 0.9 collective-permute-done.3.refs_3_
  105.8 4.6 %collective-permute-done.5.refs_1_ = bf16[8,24,384]{2,1,0:T(8,128)(2,1)S(1)} collective-permute-done((bf16[8,24,384]{2,1,0:T(8,128)(2,1)S(1)}, bf16[8,24,384]{2,1,0:T(8,128)(2,1)S(1)}, u32[]{:S(2)}, u32[]{:S(2)}) %collective-permute-start.5) | collective-permute-done | bytes 147488 | tf_op jit(solution)/shard_map/ppermute | solution.py:368
  110.4 0.7 collective-permute-done.7.refs_3_
  111.2 14.3 %all_to_all.16 = bf16[16,24,384]{2,1,0:T(8,128)(2,1)S(1)} all-to-all(bf16[16,24,384]{2,1,0:T(8,128)(2,1)S(1)} %bitcast.24), channel_id=1, replica_groups={{0,2,4,6,8,10,12,14,16,18,20,22,24,26,28,30},{1,3,5,7,9,11,13,15,17,19,..., dimensions={0} | all-to-all | bytes 589824 | tf_op jit(solution)/shard_map/all_to_all | solution.py:437
  125.6 1.5 %collective-permute-start.8 = (bf16[24,384]{1,0:T(8,128)(2,1)S(1)}, bf16[24,384]{1,0:T(8,128)(2,1)S(1)}, u32[]{:S(2)}, u32[]{:S(2)}) collective-permute-start(bf16[24,384]{1,0:T(8,128)(2,1)S(1)} %reduce_sum.12), channel_id=1, source_target_pairs={{0,128},{128,0},{1,129},{129,1},{2,130},{130,2},{3,131},{131,3},{4... | collective-permute-start | bytes 55304 | tf_op jit(solution)/shard_map/ppermute | solution.py:441
  127.1 1.8 %shard_map.104 = bf16[512,384]{1,0:T(8,128)(2,1)} custom-call(bf16[512,384]{1,0:T(8,128)(2,1)S(1)} %bitcast.27, bf16[384,1152]{1,0:T(8,128)(2,1)S(1)} %copy-done, bf16[512,1152]{1,0:T(8,128)(2,1)S(1)} %get-tuple-element.20.dcomb_ref, bf16[512,384]{1,0:T(8,128)(2,1)S(1)} %get-tuple-element.21.sg_ref), custom_call_target="tpu_custom_call" | custom-call | flops 500000000 | bytes 2850816 | tf_op jit(solution)/shard_map/pallas_call | solution.py:72
  129.5 0.6 slice_bitcast_fusion
  (25 shorter events, 2.1 us)
Async XLA Ops:
  7.8 40.2 %copy-start.2 = (bf16[384,1152]{1,0:T(8,128)(2,1)S(1)}, bf16[384,1152]{1,0:T(8,128)(2,1)}, u32[]{:S(2)}) copy-start(bf16[384,1152]{1,0:T(8,128)(2,1)} %w_ref.2) | copy-start | bytes 2654212
  7.8 40.2 %copy-start.4 = (bf16[384,384]{1,0:T(8,128)(2,1)S(1)}, bf16[384,384]{1,0:T(8,128)(2,1)}, u32[]{:S(2)}) copy-start(bf16[384,384]{1,0:T(8,128)(2,1)} %wo_ref.2) | copy-start | bytes 884740
  55.5 25.2 %all-to-all-start.1 = ((bf16[128,4,384]{2,1,0:T(4,128)(2,1)}), bf16[128,4,384]{2,1,0:T(4,128)(2,1)S(1)}, u32[]{:S(2)}, u32[]{:S(2)}) async-start(bf16[128,4,384]{2,1,0:T(4,128)(2,1)} %get-tuple-element.18), calls=%async_computation.1 | async-start | bytes 786432 | tf_op jit(solution)/shard_map/all_to_all | solution.py:454
  62.5 18.2 %copy-start.1 = (bf16[1,1,512,384]{3,2,1,0:T(8,128)(2,1)S(1)}, bf16[1,1,512,384]{3,2,1,0:T(8,128)(2,1)}, u32[]{:S(2)}) copy-start(bf16[1,1,512,384]{3,2,1,0:T(8,128)(2,1)} %param.6) | copy-start | bytes 1179652
  65.2 27.1 %collective-permute-start = (bf16[4,8,24,384]{3,2,1,0:T(8,128)(2,1)}, bf16[4,8,24,384]{3,2,1,0:T(8,128)(2,1)}, u32[]{:S(2)}, u32[]{:S(2)}) collective-permute-start(bf16[4,8,24,384]{3,2,1,0:T(8,128)(2,1)} %get-tuple-element.26), channel_id=1, source_target_pairs={{0,1},{1,0},{2,3},{3,2},{4,5},{5,4},{6,7},{7,6},{8,9},{9,8},{10,11... | collective-permute-start | bytes 1769480 | tf_op jit(solution)/shard_map/ppermute | solution.py:368
  80.7 1.0 copy-start.3
  81.7 1.0 copy-start.5
  92.0 5.2 %collective-permute-start.4 = (bf16[4,8,24,384]{3,2,1,0:T(8,128)(2,1)}, bf16[4,8,24,384]{3,2,1,0:T(8,128)(2,1)}, u32[]{:S(2)}, u32[]{:S(2)}) collective-permute-start(bf16[4,8,24,384]{3,2,1,0:T(8,128)(2,1)} %get-tuple-element.28), channel_id=1, source_target_pairs={{0,1},{1,0},{2,3},{3,2},{4,5},{5,4},{6,7},{7,6},{8,9},{9,8},{10,11... | collective-permute-start | bytes 1769480 | tf_op jit(solution)/shard_map/ppermute | solution.py:368
  93.6 11.2 %collective-permute-start.1 = (bf16[8,24,384]{2,1,0:T(8,128)(2,1)S(1)}, bf16[8,24,384]{2,1,0:T(8,128)(2,1)S(1)}, u32[]{:S(2)}, u32[]{:S(2)}) collective-permute-start(bf16[8,24,384]{2,1,0:T(8,128)(2,1)S(1)} %get-tuple-element.34), channel_id=1, source_target_pairs={{0,32},{1,33},{2,34},{3,35},{4,36},{5,37},{6,38},{7,39},{8,40},{9,... | collective-permute-start | bytes 442376 | tf_op jit(solution)/shard_map/ppermute | solution.py:368
  94.4 10.3 %collective-permute-start.2 = (bf16[8,24,384]{2,1,0:T(8,128)(2,1)S(1)}, bf16[8,24,384]{2,1,0:T(8,128)(2,1)S(1)}, u32[]{:S(2)}, u32[]{:S(2)}) collective-permute-start(bf16[8,24,384]{2,1,0:T(8,128)(2,1)S(1)} %get-tuple-element.33), channel_id=1, source_target_pairs={{0,64},{1,65},{2,66},{3,67},{4,68},{5,69},{6,70},{7,71},{8,72},{9,... | collective-permute-start | bytes 442376 | tf_op jit(solution)/shard_map/ppermute | solution.py:368
  96.1 9.6 %collective-permute-start.3 = (bf16[8,24,384]{2,1,0:T(8,128)(2,1)S(1)}, bf16[8,24,384]{2,1,0:T(8,128)(2,1)S(1)}, u32[]{:S(2)}, u32[]{:S(2)}) collective-permute-start(bf16[8,24,384]{2,1,0:T(8,128)(2,1)S(1)} %get-tuple-element.32), channel_id=1, source_target_pairs={{0,96},{1,97},{2,98},{3,99},{4,100},{5,101},{6,102},{7,103},{8,104... | collective-permute-start | bytes 442376 | tf_op jit(solution)/shard_map/ppermute | solution.py:368
  98.5 11.9 %collective-permute-start.5 = (bf16[8,24,384]{2,1,0:T(8,128)(2,1)S(1)}, bf16[8,24,384]{2,1,0:T(8,128)(2,1)S(1)}, u32[]{:S(2)}, u32[]{:S(2)}) collective-permute-start(bf16[8,24,384]{2,1,0:T(8,128)(2,1)S(1)} %get-tuple-element.31), channel_id=1, source_target_pairs={{0,32},{1,33},{2,34},{3,35},{4,36},{5,37},{6,38},{7,39},{8,40},{9,... | collective-permute-start | bytes 442376 | tf_op jit(solution)/shard_map/ppermute | solution.py:368
  99.5 10.9 %collective-permute-start.6 = (bf16[8,24,384]{2,1,0:T(8,128)(2,1)S(1)}, bf16[8,24,384]{2,1,0:T(8,128)(2,1)S(1)}, u32[]{:S(2)}, u32[]{:S(2)}) collective-permute-start(bf16[8,24,384]{2,1,0:T(8,128)(2,1)S(1)} %get-tuple-element.30), channel_id=1, source_target_pairs={{0,64},{1,65},{2,66},{3,67},{4,68},{5,69},{6,70},{7,71},{8,72},{9,... | collective-permute-start | bytes 442376 | tf_op jit(solution)/shard_map/ppermute | solution.py:368
  104.8 6.3 %collective-permute-start.7 = (bf16[8,24,384]{2,1,0:T(8,128)(2,1)S(1)}, bf16[8,24,384]{2,1,0:T(8,128)(2,1)S(1)}, u32[]{:S(2)}, u32[]{:S(2)}) collective-permute-start(bf16[8,24,384]{2,1,0:T(8,128)(2,1)S(1)} %get-tuple-element.29), channel_id=1, source_target_pairs={{0,96},{1,97},{2,98},{3,99},{4,100},{5,101},{6,102},{7,103},{8,104... | collective-permute-start | bytes 442376 | tf_op jit(solution)/shard_map/ppermute | solution.py:368
  105.8 21.3 %copy-start = (bf16[384,1152]{1,0:T(8,128)(2,1)S(1)}, bf16[384,1152]{1,0:T(8,128)(2,1)}, u32[]{:S(2)}) copy-start(bf16[384,1152]{1,0:T(8,128)(2,1)} %w_ref.3) | copy-start | bytes 2654212
  125.6 3.8 %collective-permute-start.8 = (bf16[24,384]{1,0:T(8,128)(2,1)S(1)}, bf16[24,384]{1,0:T(8,128)(2,1)S(1)}, u32[]{:S(2)}, u32[]{:S(2)}) collective-permute-start(bf16[24,384]{1,0:T(8,128)(2,1)S(1)} %reduce_sum.12), channel_id=1, source_target_pairs={{0,128},{128,0},{1,129},{129,1},{2,130},{130,2},{3,131},{131,3},{4... | collective-permute-start | bytes 55304 | tf_op jit(solution)/shard_map/ppermute | solution.py:441

commit v3 on v2

--- a/solution.py
+++ b/solution.py
@@ -63,6 +63,25 @@
     column = lax.broadcasted_iota(jnp.int32, (count, count), 1)
     source = (row & (inner - 1)) * outer + lax.shift_right_logical(row, inner.bit_length() - 1)
     return (column == source).astype(F32).astype(B16)
+
+
+def by_patch(onehot, block, patches):
+    size = onehot.shape[0]
+    some = size // patches
+    moved = [mm(onehot, block[at : at + size]) for at in range(0, block.shape[0], size)]
+    return jnp.concatenate(
+        [part[p * some : (p + 1) * some] for p in range(patches) for part in moved], 0
+    )
+
+
+def by_frame(onehot, block, patches):
+    size = onehot.shape[0]
+    some, frames = size // patches, block.shape[0] // patches
+    parts = []
+    for at in range(0, frames, some):
+        rows = [block[p * frames + at : p * frames + at + some] for p in range(patches)]
+        parts.append(mm(onehot, jnp.concatenate(rows, 0)))
+    return jnp.concatenate(parts, 0)
 
 
 HBM = pl.BlockSpec(memory_space=pltpu.HBM)
@@ -121,16 +140,25 @@
         )
     qt = (comb[:, :width] * (hw ** -0.5)).T
     vt = comb[:, 2 * width :].T
-    parts = []
-    for pair in range(HEADS // 2):
-        at = pair * 2 * hw
+
+    def scores_of(head):
+        at = head // 2 * 2 * hw
         keys = comb[:, width + at : width + at + 2 * hw]
-        for sub in range(2):
-            head = 2 * pair + sub
-            p = softmax_rows(mm(keys, one_head(qt[at : at + 2 * hw], sub, hw, 0)))
-            probs_ref[head] = p
+        return mm(keys, one_head(qt[at : at + 2 * hw], head % 2, hw, 0))
+
+    parts, probs = [], []
+    ahead = scores_of(0)
+    for head in range(HEADS + 1):
+        if head < HEADS:
+            scores = ahead
+            if head + 1 < HEADS:
+                ahead = scores_of(head + 1)
+            probs.append(softmax_rows(scores))
+            probs_ref[head] = probs[head]
             outs.append(copies.start(probs_ref.at[head], saved_hbm.at[head]))
-            parts.append(mm(vt[head * hw : (head + 1) * hw], p).astype(B16))
+        if head:
+            own = slice((head - 1) * hw, head * hw)
+            parts.append(mm(vt[own], probs[head - 1]).astype(B16))
     att = jnp.concatenate(parts, 0).T
     wide_ref[:, 3 * width :] = att
     outs.append(copies.start(wide_ref.at[:, 2 * rows :], saved_hbm.at[HEADS + 2]))
@@ -161,9 +189,10 @@
     frames, _, patches, width = slab_ref.shape
     rows = frames * patches
     hw = width // HEADS
-    gather = regroup(rows, frames, patches)
-    x = mm(gather, slab_ref[:, 0].reshape(rows, width))
-    cot = mm(gather, slab_ref[:, 1].reshape(rows, width)).astype(B16)
+    size = min(rows, 256)
+    gather = regroup(size, size // patches, patches)
+    x = by_patch(gather, slab_ref[:, 0].reshape(rows, width), patches)
+    cot = by_patch(gather, slab_ref[:, 1].reshape(rows, width), patches).astype(B16)
     scaled, inverse = normalize(x)
     normed = scaled.astype(B16)
     normed_ref[...] = normed
@@ -173,26 +202,33 @@
     k = comb[:, width : 2 * width]
     v = comb[:, 2 * width :]
     qt, kt, vt, gt = q.T, k.T, v.T, g.T
-    dqt_parts, att_parts, dk_parts, dv_parts = [], [], [], []
-    for patch in range(patches):
-        here = slice(patch * frames, (patch + 1) * frames)
-        dqt_p, att_p, dk_p, dv_p = [], [], [], []
-        for pair in range(HEADS // 2):
-            lanes = slice(pair * 2 * hw, (pair + 1) * 2 * hw)
-            p = softmax_rows(mm(k[here, lanes], both_heads(qt[lanes, here], hw, 0, 1)))
-            dp = mm(v[here, lanes], both_heads(gt[lanes, here], hw, 0, 1))
-            ds = score_back(p, dp)
-            for sub in range(2):
-                own = slice((2 * pair + sub) * hw, (2 * pair + sub + 1) * hw)
-                cols = slice(sub * frames, (sub + 1) * frames)
-                att_p.append(mm(vt[own, here], p[:, cols]).astype(B16))
-                dqt_p.append((mm(kt[own, here], ds[:, cols]) * (hw ** -0.5)).astype(B16))
-            dk_p.append(mm(ds, both_heads(q[here, lanes], hw, 1, 0)).astype(B16))
-            dv_p.append(mm(p, both_heads(g[here, lanes], hw, 1, 0)).astype(B16))
-        dqt_parts.append(jnp.concatenate(dqt_p, 0))
-        att_parts.append(jnp.concatenate(att_p, 0))
-        dk_parts.append(jnp.concatenate(dk_p, 1))
-        dv_parts.append(jnp.concatenate(dv_p, 1))
+    groups = [
+        (slice(patch * frames, (patch + 1) * frames), slice(pair * 2 * hw, (pair + 1) * 2 * hw))
+        for patch in range(patches)
+        for pair in range(HEADS // 2)
+    ]
+    scores = [mm(k[here, lanes], both_heads(qt[lanes, here], hw, 0, 1)) for here, lanes in groups]
+    back = [mm(v[here, lanes], both_heads(gt[lanes, here], hw, 0, 1)) for here, lanes in groups]
+    probs = [softmax_rows(member) for member in scores]
+    grads = [score_back(p, dp) for p, dp in zip(probs, back)]
+    dk = [mm(ds, both_heads(q[at], hw, 1, 0)).astype(B16) for ds, at in zip(grads, groups)]
+    dv = [mm(p, both_heads(g[at], hw, 1, 0)).astype(B16) for p, at in zip(probs, groups)]
+    att, dqt = [], []
+    for p, ds, (here, lanes) in zip(probs, grads, groups):
+        for sub in range(2):
+            own = slice(lanes.start + sub * hw, lanes.start + (sub + 1) * hw)
+            cols = slice(sub * frames, (sub + 1) * frames)
+            att.append(mm(vt[own, here], p[:, cols]).astype(B16))
+            dqt.append((mm(kt[own, here], ds[:, cols]) * (hw ** -0.5)).astype(B16))
+
+    def by_patch_of(parts, axis):
+        each = len(parts) // patches
+        return [
+            jnp.concatenate(parts[n * each : (n + 1) * each], axis) for n in range(patches)
+        ]
+
+    dqt_parts, att_parts = by_patch_of(dqt, 0), by_patch_of(att, 0)
+    dk_parts, dv_parts = by_patch_of(dk, 1), by_patch_of(dv, 1)
     dqt = jnp.concatenate(dqt_parts, 1)
     att = jnp.concatenate(att_parts, 1).T
     go_ref[...] = (mm(cot.T, att) * factor).astype(B16)
@@ -207,8 +243,9 @@
         + mm(dv, w_ref[:, 2 * width :], NT)
     )
     branch = normalize_back(scaled, inverse, u).astype(B16)
-    scatter = regroup(rows, patches, frames)
-    branch_ref[...] = mm(scatter, branch).astype(B16).reshape(branch_ref.shape)
+    scatter = regroup(size, patches, size // patches)
+    branch = by_frame(scatter, branch, patches).astype(B16)
+    branch_ref[...] = branch.reshape(branch_ref.shape)
 
 
 def temporal(factor, slab, w, wo):
@@ -287,21 +324,33 @@
         copy.wait()
     q = comb_ref[:, :width] * (hw ** -0.5)
     kt = comb_ref[:, width : 2 * width].T
-    dqt_parts, dk_parts, dv_parts = [], [], []
-    for pair in range(HEADS // 2):
-        lanes = slice(pair * 2 * hw, (pair + 1) * 2 * hw)
-        values = comb_ref[:, 2 * width + pair * 2 * hw : 2 * width + (pair + 1) * 2 * hw]
-        dk = dv = 0.0
-        for sub in range(2):
-            head = 2 * pair + sub
-            p = probs_ref[head]
-            ds = score_back(p, mm(values, one_head(gt[lanes], sub, hw, 0)))
-            dqt = mm(kt[head * hw : (head + 1) * hw], ds) * (hw ** -0.5)
-            dqt_parts.append(dqt.astype(B16))
-            dk = dk + mm(ds, one_head(q[:, lanes], sub, hw, 1))
-            dv = dv + mm(p, one_head(g[:, lanes], sub, hw, 1))
-        dk_parts.append(dk.astype(B16))
-        dv_parts.append(dv.astype(B16))
+
+    def back_of(head):
+        at = head // 2 * 2 * hw
+        values = comb_ref[:, 2 * width + at : 2 * width + at + 2 * hw]
+        return mm(values, one_head(gt[at : at + 2 * hw], head % 2, hw, 0))
+
+    dqt_parts, dk_parts, dv_parts, grads = [], [], [], []
+    ahead = back_of(0)
+    for step in range(HEADS + 1):
+        if step < HEADS:
+            dp = ahead
+            if step + 1 < HEADS:
+                ahead = back_of(step + 1)
+            grads.append(score_back(probs_ref[step], dp))
+        if not step:
+            continue
+        head, sub = step - 1, (step - 1) % 2
+        lanes = slice(head // 2 * 2 * hw, (head // 2 + 1) * 2 * hw)
+        ds = grads[head]
+        dqt = mm(kt[head * hw : (head + 1) * hw], ds) * (hw ** -0.5)
+        dqt_parts.append(dqt.astype(B16))
+        dk = mm(ds, one_head(q[:, lanes], sub, hw, 1))
+        dv = mm(probs_ref[head], one_head(g[:, lanes], sub, hw, 1))
+        if sub:
+            dk_parts.append((dk_first + dk).astype(B16))
+            dv_parts.append((dv_first + dv).astype(B16))
+        dk_first, dv_first = dk, dv
     dqt = jnp.concatenate(dqt_parts, 0)
     dk = jnp.concatenate(dk_parts, 1)
     dv = jnp.concatenate(dv_parts, 1)

time: 133 us -> 129 us (0.970)
  Pallas kernels: 28.7 us -> 25.3 us
    pallas_call x7, Pallas kernels: 28.7 us -> 25.3 us  [call(): pl.pallas_call(kernel, out_shape=tuple((jax.ShapeDtypeStruct(shape, B16)...]
where the time goes in v3:
time: 129 us; the launch traced here: 127 us
  blocking collectives  54.6 us (42%)
  Pallas kernels  25.3 us (20%)
  waiting for transfers between devices  25.2 us (20%)
  starting transfers between devices  15.6 us (12%)
  local copies, waits for them, and re-layouts  3.32 us (3%)
  other arithmetic  2.47 us (2%)
    all_to_all x1, blocking collectives, trade(): return lax.all_to_all(array, 'seq', split_axis=0, concat_axis=0, tiled=True)  40.2 us
    pallas_call x7, Pallas kernels, call(): pl.pallas_call(kernel, out_shape=tuple((jax.ShapeDtypeStruct(shape, B16)...  25.3 us
    all_to_all x1, waiting for transfers between devices, trade(): return lax.all_to_all(array, 'seq', split_axis=0, concat_axis=0, tiled=True)  15.2 us
    all_to_all x1, blocking collectives, last_stages(): lax.all_to_all(flat, 'seq', split_axis=0, concat_axis=0, tiled=True, axis...  14.4 us
    ppermute x8, waiting for transfers between devices, shift(): return lax.ppermute(array, 'seq', pairs)  9.6 us
    all_to_all x1, starting transfers between devices, trade(): return lax.all_to_all(array, 'seq', split_axis=0, concat_axis=0, tiled=True)  7.24 us
    ppermute x8, starting transfers between devices, shift(): return lax.ppermute(array, 'seq', pairs)  6.87 us
  transfers between devices with their start and end apart: 10, of which 6 were waited for; matrix products, arithmetic and copies ran while one was open for 2% of the time, Pallas kernels for 11%

profile of v3, /device:TPU:8, one launch (start us, length us, event | category | flops | bytes accessed | tf_op | source)
XLA Modules:
  0.0 127.3 jit_solution(4632734712471528659)
XLA Ops:
  0.6 6.3 %shard_map.101 = (bf16[128,2,4,384]{3,2,1,0:T(4,128)(2,1)}, bf16[9,512,512]{2,1,0:T(8,128)(2,1)}) custom-call(bf16[512,384]{1,0:T(8,128)(2,1)} %bitcast.25, bf16[512,384]{1,0:T(8,128)(2,1)} %bitcast.28, bf16[384,1152]{1,0:T(8,128)(2,1)} %w_ref.3, bf16[384,384]{1,0:T(8,128)(2,1)} %wo_ref.3), custom_call_target="tpu_custom_call" | custom-call | flops 2000000000 | bytes 1966080 | tf_op jit(solution)/shard_map/pallas_call | solution.py:91
  6.9 40.2 %all_to_all.15.slab_ref = bf16[128,2,4,384]{3,2,1,0:T(4,128)(2,1)S(1)} all-to-all(bf16[128,2,4,384]{3,2,1,0:T(4,128)(2,1)} %get-tuple-element.17), channel_id=1, replica_groups=mesh['dp'=2,'seq'=128] {'seq'}, dimensions={0} | all-to-all | bytes 1572864 | tf_op jit(solution)/shard_map/all_to_all | solution.py:503
  47.1 5.5 %shard_map.102 = (bf16[128,4,384]{2,1,0:T(4,128)(2,1)}, bf16[512,384]{1,0:T(8,128)(2,1)S(1)}, bf16[384,384]{1,0:T(8,128)(2,1)S(1)}, bf16[1152,512]{1,0:T(8,128)(2,1)S(1)}) custom-call(bf16[128,2,4,384]{3,2,1,0:T(4,128)(2,1)S(1)} %all_to_all.15.slab_ref, bf16[384,1152]{1,0:T(8,128)(2,1)S(1)} %copy-done.2, bf16[384,384]{1,0:T(8,128)(2,1)S(1)} %copy-done.4), custom_call_target="tpu_custom_call" | custom-call | flops 3000000000 | bytes 1966080 | tf_op jit(solution)/shard_map/pallas_call | solution.py:91
  52.6 7.2 %all-to-all-start.1 = ((bf16[128,4,384]{2,1,0:T(4,128)(2,1)}), bf16[128,4,384]{2,1,0:T(4,128)(2,1)S(1)}, u32[]{:S(2)}, u32[]{:S(2)}) async-start(bf16[128,4,384]{2,1,0:T(4,128)(2,1)} %get-tuple-element.18), calls=%async_computation.1 | async-start | bytes 786432 | tf_op jit(solution)/shard_map/all_to_all | solution.py:503
  59.9 2.7 %shard_map.105 = (bf16[4,8,24,384]{3,2,1,0:T(8,128)(2,1)S(1)}, bf16[4,8,24,384]{3,2,1,0:T(8,128)(2,1)}) custom-call(bf16[512,384]{1,0:T(8,128)(2,1)S(1)} %get-tuple-element.22.normed_ref, bf16[384,384]{1,0:T(8,128)(2,1)S(1)} %get-tuple-element.23.go_ref, bf16[1152,512]{1,0:T(8,128)(2,1)S(1)} %get-tuple-element.24.dct_ref), custom_call_target="tpu_custom_call" | custom-call | flops 1500000000 | bytes 1867776 | tf_op jit(solution)/shard_map/pallas_call | solution.py:91
  62.7 15.2 %all-to-all-done.1.br_ref = bf16[128,4,384]{2,1,0:T(4,128)(2,1)S(1)} async-done(((bf16[128,4,384]{2,1,0:T(4,128)(2,1)}), bf16[128,4,384]{2,1,0:T(4,128)(2,1)S(1)}, u32[]{:S(2)}, u32[]{:S(2)}) %all-to-all-start.1) | async-done | bytes 393248 | tf_op jit(solution)/shard_map/all_to_all | solution.py:503
  77.9 1.0 copy-done.3
  78.8 1.0 copy-done.5
  79.8 8.7 %shard_map.103 = (bf16[4,8,24,384]{3,2,1,0:T(8,128)(2,1)S(1)}, bf16[4,8,24,384]{3,2,1,0:T(8,128)(2,1)}, bf16[512,384]{1,0:T(8,128)(2,1)S(1)}, bf16[512,1152]{1,0:T(8,128)(2,1)S(1)}) custom-call(bf16[512,384]{1,0:T(8,128)(2,1)S(1)} %bitcast.29, bf16[128,4,384]{2,1,0:T(4,128)(2,1)S(1)} %all-to-all-done.1.br_ref, bf16[384,384]{1,0:T(8,128)(2,1)S(1)} %copy-done.5, ...), custom_call_target="tpu_custom_call" | custom-call | flops 4000000000 | bytes 6193152 | tf_op jit(solution)/shard_map/pallas_call | solution.py:91
  88.8 1.2 add_convert_fusion.1.refs_0_
  90.1 0.9 collective-permute-start.1
  91.0 1.6 %collective-permute-start.2 = (bf16[8,24,384]{2,1,0:T(8,128)(2,1)S(1)}, bf16[8,24,384]{2,1,0:T(8,128)(2,1)S(1)}, u32[]{:S(2)}, u32[]{:S(2)}) collective-permute-start(bf16[8,24,384]{2,1,0:T(8,128)(2,1)S(1)} %get-tuple-element.33), channel_id=1, source_target_pairs={{0,64},{1,65},{2,66},{3,67},{4,68},{5,69},{6,70},{7,71},{8,72},{9,... | collective-permute-start | bytes 442376 | tf_op jit(solution)/shard_map/ppermute | solution.py:417
  92.6 1.1 collective-permute-start.3
  93.8 1.2 add_convert_fusion.refs_0_
  95.0 1.0 collective-permute-start.5
  96.0 1.9 %collective-permute-start.6 = (bf16[8,24,384]{2,1,0:T(8,128)(2,1)S(1)}, bf16[8,24,384]{2,1,0:T(8,128)(2,1)S(1)}, u32[]{:S(2)}, u32[]{:S(2)}) collective-permute-start(bf16[8,24,384]{2,1,0:T(8,128)(2,1)S(1)} %get-tuple-element.30), channel_id=1, source_target_pairs={{0,64},{1,65},{2,66},{3,67},{4,68},{5,69},{6,70},{7,71},{8,72},{9,... | collective-permute-start | bytes 442376 | tf_op jit(solution)/shard_map/ppermute | solution.py:417
  97.9 3.4 %collective-permute-done.1.refs_1_ = bf16[8,24,384]{2,1,0:T(8,128)(2,1)S(1)} collective-permute-done((bf16[8,24,384]{2,1,0:T(8,128)(2,1)S(1)}, bf16[8,24,384]{2,1,0:T(8,128)(2,1)S(1)}, u32[]{:S(2)}, u32[]{:S(2)}) %collective-permute-start.1) | collective-permute-done | bytes 147488 | tf_op jit(solution)/shard_map/ppermute | solution.py:417
  101.3 0.9 collective-permute-done.3.refs_3_
  102.3 4.6 %collective-permute-done.5.refs_1_ = bf16[8,24,384]{2,1,0:T(8,128)(2,1)S(1)} collective-permute-done((bf16[8,24,384]{2,1,0:T(8,128)(2,1)S(1)}, bf16[8,24,384]{2,1,0:T(8,128)(2,1)S(1)}, u32[]{:S(2)}, u32[]{:S(2)}) %collective-permute-start.5) | collective-permute-done | bytes 147488 | tf_op jit(solution)/shard_map/ppermute | solution.py:417
  107.0 0.7 collective-permute-done.7.refs_3_
  107.8 14.4 %all_to_all.16 = bf16[16,24,384]{2,1,0:T(8,128)(2,1)S(1)} all-to-all(bf16[16,24,384]{2,1,0:T(8,128)(2,1)S(1)} %bitcast.24), channel_id=1, replica_groups={{0,2,4,6,8,10,12,14,16,18,20,22,24,26,28,30},{1,3,5,7,9,11,13,15,17,19,..., dimensions={0} | all-to-all | bytes 589824 | tf_op jit(solution)/shard_map/all_to_all | solution.py:486
  122.2 1.5 %collective-permute-start.8 = (bf16[24,384]{1,0:T(8,128)(2,1)S(1)}, bf16[24,384]{1,0:T(8,128)(2,1)S(1)}, u32[]{:S(2)}, u32[]{:S(2)}) collective-permute-start(bf16[24,384]{1,0:T(8,128)(2,1)S(1)} %reduce_sum.12), channel_id=1, source_target_pairs={{0,128},{128,0},{1,129},{129,1},{2,130},{130,2},{3,131},{131,3},{4... | collective-permute-start | bytes 55304 | tf_op jit(solution)/shard_map/ppermute | solution.py:490
  123.7 1.8 %shard_map.104 = bf16[512,384]{1,0:T(8,128)(2,1)} custom-call(bf16[512,384]{1,0:T(8,128)(2,1)S(1)} %bitcast.27, bf16[384,1152]{1,0:T(8,128)(2,1)S(1)} %copy-done, bf16[512,1152]{1,0:T(8,128)(2,1)S(1)} %get-tuple-element.20.dcomb_ref, bf16[512,384]{1,0:T(8,128)(2,1)S(1)} %get-tuple-element.21.sg_ref), custom_call_target="tpu_custom_call" | custom-call | flops 500000000 | bytes 2850816 | tf_op jit(solution)/shard_map/pallas_call | solution.py:91
  126.0 0.6 slice_bitcast_fusion
  (25 shorter events, 1.9 us)
Async XLA Ops:
  6.9 40.2 %copy-start.2 = (bf16[384,1152]{1,0:T(8,128)(2,1)S(1)}, bf16[384,1152]{1,0:T(8,128)(2,1)}, u32[]{:S(2)}) copy-start(bf16[384,1152]{1,0:T(8,128)(2,1)} %w_ref.2) | copy-start | bytes 2654212
  6.9 40.2 %copy-start.4 = (bf16[384,384]{1,0:T(8,128)(2,1)S(1)}, bf16[384,384]{1,0:T(8,128)(2,1)}, u32[]{:S(2)}) copy-start(bf16[384,384]{1,0:T(8,128)(2,1)} %wo_ref.2) | copy-start | bytes 884740
  52.6 25.2 %all-to-all-start.1 = ((bf16[128,4,384]{2,1,0:T(4,128)(2,1)}), bf16[128,4,384]{2,1,0:T(4,128)(2,1)S(1)}, u32[]{:S(2)}, u32[]{:S(2)}) async-start(bf16[128,4,384]{2,1,0:T(4,128)(2,1)} %get-tuple-element.18), calls=%async_computation.1 | async-start | bytes 786432 | tf_op jit(solution)/shard_map/all_to_all | solution.py:503
  59.9 18.0 %copy-start.1 = (bf16[1,1,512,384]{3,2,1,0:T(8,128)(2,1)S(1)}, bf16[1,1,512,384]{3,2,1,0:T(8,128)(2,1)}, u32[]{:S(2)}) copy-start(bf16[1,1,512,384]{3,2,1,0:T(8,128)(2,1)} %param.6) | copy-start | bytes 1179652
  62.6 26.2 %collective-permute-start = (bf16[4,8,24,384]{3,2,1,0:T(8,128)(2,1)}, bf16[4,8,24,384]{3,2,1,0:T(8,128)(2,1)}, u32[]{:S(2)}, u32[]{:S(2)}) collective-permute-start(bf16[4,8,24,384]{3,2,1,0:T(8,128)(2,1)} %get-tuple-element.26), channel_id=1, source_target_pairs={{0,1},{1,0},{2,3},{3,2},{4,5},{5,4},{6,7},{7,6},{8,9},{9,8},{10,11... | collective-permute-start | bytes 1769480 | tf_op jit(solution)/shard_map/ppermute | solution.py:417
  77.8 1.0 copy-start.3
  78.8 1.0 copy-start.5
  88.6 5.2 %collective-permute-start.4 = (bf16[4,8,24,384]{3,2,1,0:T(8,128)(2,1)}, bf16[4,8,24,384]{3,2,1,0:T(8,128)(2,1)}, u32[]{:S(2)}, u32[]{:S(2)}) collective-permute-start(bf16[4,8,24,384]{3,2,1,0:T(8,128)(2,1)} %get-tuple-element.28), channel_id=1, source_target_pairs={{0,1},{1,0},{2,3},{3,2},{4,5},{5,4},{6,7},{7,6},{8,9},{9,8},{10,11... | collective-permute-start | bytes 1769480 | tf_op jit(solution)/shard_map/ppermute | solution.py:417
  90.1 11.2 %collective-permute-start.1 = (bf16[8,24,384]{2,1,0:T(8,128)(2,1)S(1)}, bf16[8,24,384]{2,1,0:T(8,128)(2,1)S(1)}, u32[]{:S(2)}, u32[]{:S(2)}) collective-permute-start(bf16[8,24,384]{2,1,0:T(8,128)(2,1)S(1)} %get-tuple-element.34), channel_id=1, source_target_pairs={{0,32},{1,33},{2,34},{3,35},{4,36},{5,37},{6,38},{7,39},{8,40},{9,... | collective-permute-start | bytes 442376 | tf_op jit(solution)/shard_map/ppermute | solution.py:417
  91.0 10.3 %collective-permute-start.2 = (bf16[8,24,384]{2,1,0:T(8,128)(2,1)S(1)}, bf16[8,24,384]{2,1,0:T(8,128)(2,1)S(1)}, u32[]{:S(2)}, u32[]{:S(2)}) collective-permute-start(bf16[8,24,384]{2,1,0:T(8,128)(2,1)S(1)} %get-tuple-element.33), channel_id=1, source_target_pairs={{0,64},{1,65},{2,66},{3,67},{4,68},{5,69},{6,70},{7,71},{8,72},{9,... | collective-permute-start | bytes 442376 | tf_op jit(solution)/shard_map/ppermute | solution.py:417
  92.6 9.6 %collective-permute-start.3 = (bf16[8,24,384]{2,1,0:T(8,128)(2,1)S(1)}, bf16[8,24,384]{2,1,0:T(8,128)(2,1)S(1)}, u32[]{:S(2)}, u32[]{:S(2)}) collective-permute-start(bf16[8,24,384]{2,1,0:T(8,128)(2,1)S(1)} %get-tuple-element.32), channel_id=1, source_target_pairs={{0,96},{1,97},{2,98},{3,99},{4,100},{5,101},{6,102},{7,103},{8,104... | collective-permute-start | bytes 442376 | tf_op jit(solution)/shard_map/ppermute | solution.py:417
  95.0 11.9 %collective-permute-start.5 = (bf16[8,24,384]{2,1,0:T(8,128)(2,1)S(1)}, bf16[8,24,384]{2,1,0:T(8,128)(2,1)S(1)}, u32[]{:S(2)}, u32[]{:S(2)}) collective-permute-start(bf16[8,24,384]{2,1,0:T(8,128)(2,1)S(1)} %get-tuple-element.31), channel_id=1, source_target_pairs={{0,32},{1,33},{2,34},{3,35},{4,36},{5,37},{6,38},{7,39},{8,40},{9,... | collective-permute-start | bytes 442376 | tf_op jit(solution)/shard_map/ppermute | solution.py:417
  96.0 11.0 %collective-permute-start.6 = (bf16[8,24,384]{2,1,0:T(8,128)(2,1)S(1)}, bf16[8,24,384]{2,1,0:T(8,128)(2,1)S(1)}, u32[]{:S(2)}, u32[]{:S(2)}) collective-permute-start(bf16[8,24,384]{2,1,0:T(8,128)(2,1)S(1)} %get-tuple-element.30), channel_id=1, source_target_pairs={{0,64},{1,65},{2,66},{3,67},{4,68},{5,69},{6,70},{7,71},{8,72},{9,... | collective-permute-start | bytes 442376 | tf_op jit(solution)/shard_map/ppermute | solution.py:417
  101.3 6.3 %collective-permute-start.7 = (bf16[8,24,384]{2,1,0:T(8,128)(2,1)S(1)}, bf16[8,24,384]{2,1,0:T(8,128)(2,1)S(1)}, u32[]{:S(2)}, u32[]{:S(2)}) collective-permute-start(bf16[8,24,384]{2,1,0:T(8,128)(2,1)S(1)} %get-tuple-element.29), channel_id=1, source_target_pairs={{0,96},{1,97},{2,98},{3,99},{4,100},{5,101},{6,102},{7,103},{8,104... | collective-permute-start | bytes 442376 | tf_op jit(solution)/shard_map/ppermute | solution.py:417
  102.3 21.4 %copy-start = (bf16[384,1152]{1,0:T(8,128)(2,1)S(1)}, bf16[384,1152]{1,0:T(8,128)(2,1)}, u32[]{:S(2)}) copy-start(bf16[384,1152]{1,0:T(8,128)(2,1)} %w_ref.3) | copy-start | bytes 2654212
  122.2 3.8 %collective-permute-start.8 = (bf16[24,384]{1,0:T(8,128)(2,1)S(1)}, bf16[24,384]{1,0:T(8,128)(2,1)S(1)}, u32[]{:S(2)}, u32[]{:S(2)}) collective-permute-start(bf16[24,384]{1,0:T(8,128)(2,1)S(1)} %reduce_sum.12), channel_id=1, source_target_pairs={{0,128},{128,0},{1,129},{129,1},{2,130},{130,2},{3,131},{131,3},{4... | collective-permute-start | bytes 55304 | tf_op jit(solution)/shard_map/ppermute | solution.py:490

commit v4 on v3

--- a/solution.py
+++ b/solution.py
@@ -302,7 +302,7 @@
 
 def spatial_backward_kernel(
     factor, ct_ref, br_ref, wo_ref, saved_hbm, tok_ref,
-    own_ref, send_ref, sg_ref, dcomb_ref,
+    own_ref, send_ref, sg_ref, dqt_ref, dkv_ref,
     comb_ref, probs_ref, slab_ref, sems,
 ):
     copies = Copies(sems)
@@ -320,8 +320,9 @@
     gt = g.T
     scaled, _ = normalize(tok_ref[...].astype(F32))
     normed = scaled.astype(B16)
-    for copy in comb_in + probs_in:
+    for copy in comb_in:
         copy.wait()
+    go = (mm(sg.T, comb_ref[:, 3 * width :]) * factor).astype(B16)
     q = comb_ref[:, :width] * (hw ** -0.5)
     kt = comb_ref[:, width : 2 * width].T
 
@@ -332,6 +333,8 @@
 
     dqt_parts, dk_parts, dv_parts, grads = [], [], [], []
     ahead = back_of(0)
+    for copy in probs_in:
+        copy.wait()
     for step in range(HEADS + 1):
         if step < HEADS:
             dp = ahead
@@ -356,35 +359,35 @@
     dv = jnp.concatenate(dv_parts, 1)
     dct = jnp.concatenate([dqt, dk.T, dv.T], 0)
     gq = (mm(dct, normed) * factor).astype(B16)
-    go = (mm(sg.T, comb_ref[:, 3 * width :]) * factor).astype(B16)
     spread(gq, go, slab_ref, own_ref, send_ref)
-    dcomb_ref[:, :width] = dqt.T
-    dcomb_ref[:, width : 2 * width] = dk
-    dcomb_ref[:, 2 * width :] = dv
+    dqt_ref[...] = dqt
+    dkv_ref[:, :width] = dk
+    dkv_ref[:, width:] = dv
 
 
 def spatial_backward(factor, ct, branch, wo, saved, tokens, shape):
     rows, width = tokens.shape
     arrays = (ct, branch, wo, saved, tokens)
-    square, wide = (rows, width), (rows, 3 * width)
+    square, wide = (rows, width), (rows, 2 * width)
     return call(
         functools.partial(spatial_backward_kernel, factor), arrays,
-        (shape[1:], shape[1:], square, wide),
-        [VM, VM, VM, HBM, VM], [VM] * 4,
+        (shape[1:], shape[1:], square, (width, rows), wide),
+        [VM, VM, VM, HBM, VM], [VM] * 5,
         [(rows, 4 * width), (HEADS, rows, rows), shape], 3 + HEADS, 4_000_000_000, 0, 48,
     )
 
 
-def token_kernel(tok_ref, w_ref, dcomb_ref, sg_ref, out_ref, _):
+def token_kernel(tok_ref, w_ref, dqt_ref, dkv_ref, sg_ref, out_ref, _):
+    width = tok_ref.shape[1]
     scaled, inverse = normalize(tok_ref[...].astype(F32))
-    u = mm(dcomb_ref[...], w_ref[...], NT)
+    u = mm(dqt_ref[...].T, w_ref[:, :width], NT) + mm(dkv_ref[...], w_ref[:, width:], NT)
     out_ref[...] = (sg_ref[...].astype(F32) + normalize_back(scaled, inverse, u)).astype(B16)
 
 
-def token_gradient(tokens, w, dcomb, sg):
-    return call(
-        token_kernel, (tokens, w, dcomb, sg), (tokens.shape,),
-        [VM] * 4, [VM], [], 1, 500_000_000, 0, 48,
+def token_gradient(tokens, w, dqt, dkv, sg):
+    return call(
+        token_kernel, (tokens, w, dqt, dkv, sg), (tokens.shape,),
+        [VM] * 5, [VM], [], 1, 500_000_000, 0, 48,
     )[0]
 
 
@@ -507,11 +510,11 @@
     branch = trade(branch)
     own, send = weight_slabs(factor, normed_t, go_t, dct, shape)
     half_t = first_stages(own, send)
-    own, send, stream_grad, dcomb = spatial_backward(
+    own, send, stream_grad, dqt, dkv = spatial_backward(
         factor, cot, branch, wo_spatial, saved, tok, shape
     )
     half_s = first_stages(own, send)
-    token_grad = token_gradient(tok, wqkv_spatial, dcomb, stream_grad)
+    token_grad = token_gradient(tok, wqkv_spatial, dqt, dkv, stream_grad)
     half_t = sum_early(half_t)
     joined = join(half_t, half_s)
     own = last_stages(joined)

time: 129 us -> 131 us (1.016)
  local copies, waits for them, and re-layouts: 3.32 us -> 6.4 us
  waiting for transfers between devices: 25.2 us -> 23.8 us
    unnamed x12 -> x20, local copies, waits for them, and re-layouts: 1.98 us -> 5.06 us
  transfers between devices with their start and end apart: 10 -> 10, of which waited for: 6 -> 6; matrix products, arithmetic and copies ran while one was open for 2% -> 2% of each run, Pallas kernels for 11% -> 10%
where the time goes in v4:
time: 131 us; the launch traced here: 129 us
  blocking collectives  54.6 us (42%)
  Pallas kernels  25.2 us (19%)
  waiting for transfers between devices  23.8 us (18%)
  starting transfers between devices  15.8 us (12%)
  local copies, waits for them, and re-layouts  6.4 us (5%)
  other arithmetic  2.47 us (2%)
    all_to_all x1, blocking collectives, trade(): return lax.all_to_all(array, 'seq', split_axis=0, concat_axis=0, tiled=True)  40.2 us
    pallas_call x7, Pallas kernels, call(): pl.pallas_call(kernel, out_shape=tuple((jax.ShapeDtypeStruct(shape, B16)...  25.2 us
    all_to_all x1, blocking collectives, last_stages(): lax.all_to_all(flat, 'seq', split_axis=0, concat_axis=0, tiled=True, axis...  14.4 us
    all_to_all x1, waiting for transfers between devices, trade(): return lax.all_to_all(array, 'seq', split_axis=0, concat_axis=0, tiled=True)  13.9 us
    ppermute x8, waiting for transfers between devices, shift(): return lax.ppermute(array, 'seq', pairs)  9.46 us
    all_to_all x1, starting transfers between devices, trade(): return lax.all_to_all(array, 'seq', split_axis=0, concat_axis=0, tiled=True)  7.22 us
    ppermute x8, starting transfers between devices, shift(): return lax.ppermute(array, 'seq', pairs)  7.02 us
    unnamed x20, local copies, waits for them, and re-layouts  5.06 us
  transfers between devices with their start and end apart: 10, of which 6 were waited for; matrix products, arithmetic and copies ran while one was open for 2% of the time, Pallas kernels for 10%

profile of v4, /device:TPU:8, one launch (start us, length us, event | category | flops | bytes accessed | tf_op | source)
XLA Modules:
  0.0 129.0 jit_solution(10675182983898731936)
XLA Ops:
  0.6 6.3 %shard_map.101 = (bf16[128,2,4,384]{3,2,1,0:T(4,128)(2,1)}, bf16[9,512,512]{2,1,0:T(8,128)(2,1)}) custom-call(bf16[512,384]{1,0:T(8,128)(2,1)} %bitcast.25, bf16[512,384]{1,0:T(8,128)(2,1)} %bitcast.28, bf16[384,1152]{1,0:T(8,128)(2,1)} %w_ref.3, bf16[384,384]{1,0:T(8,128)(2,1)} %wo_ref.3), custom_call_target="tpu_custom_call" | custom-call | flops 2000000000 | bytes 1966080 | tf_op jit(solution)/shard_map/pallas_call | solution.py:91
  6.9 40.2 %all_to_all.15.slab_ref = bf16[128,2,4,384]{3,2,1,0:T(4,128)(2,1)S(1)} all-to-all(bf16[128,2,4,384]{3,2,1,0:T(4,128)(2,1)} %get-tuple-element.18), channel_id=1, replica_groups=mesh['dp'=2,'seq'=128] {'seq'}, dimensions={0} | all-to-all | bytes 1572864 | tf_op jit(solution)/shard_map/all_to_all | solution.py:506
  47.1 5.5 %shard_map.102 = (bf16[128,4,384]{2,1,0:T(4,128)(2,1)}, bf16[512,384]{1,0:T(8,128)(2,1)S(1)}, bf16[384,384]{1,0:T(8,128)(2,1)S(1)}, bf16[1152,512]{1,0:T(8,128)(2,1)S(1)}) custom-call(bf16[128,2,4,384]{3,2,1,0:T(4,128)(2,1)S(1)} %all_to_all.15.slab_ref, bf16[384,1152]{1,0:T(8,128)(2,1)S(1)} %copy-done.4, bf16[384,384]{1,0:T(8,128)(2,1)S(1)} %copy-done.6), custom_call_target="tpu_custom_call" | custom-call | flops 3000000000 | bytes 1966080 | tf_op jit(solution)/shard_map/pallas_call | solution.py:91
  52.6 1.0 copy-done.8
  53.7 7.2 %all-to-all-start.1 = ((bf16[128,4,384]{2,1,0:T(4,128)(2,1)}), bf16[128,4,384]{2,1,0:T(4,128)(2,1)S(1)}, u32[]{:S(2)}, u32[]{:S(2)}) async-start(bf16[128,4,384]{2,1,0:T(4,128)(2,1)} %get-tuple-element.19), calls=%async_computation.1 | async-start | bytes 786432 | tf_op jit(solution)/shard_map/all_to_all | solution.py:506
  60.9 1.3 copy-done.9
  62.2 2.7 %shard_map.105 = (bf16[4,8,24,384]{3,2,1,0:T(8,128)(2,1)S(1)}, bf16[4,8,24,384]{3,2,1,0:T(8,128)(2,1)}) custom-call(bf16[512,384]{1,0:T(8,128)(2,1)S(1)} %get-tuple-element.24.normed_ref, bf16[384,384]{1,0:T(8,128)(2,1)S(1)} %get-tuple-element.25.go_ref, bf16[1152,512]{1,0:T(8,128)(2,1)S(1)} %copy-done.9), custom_call_target="tpu_custom_call" | custom-call | flops 1500000000 | bytes 1867776 | tf_op jit(solution)/shard_map/pallas_call | solution.py:91
  65.0 13.9 %all-to-all-done.1.br_ref = bf16[128,4,384]{2,1,0:T(4,128)(2,1)S(1)} async-done(((bf16[128,4,384]{2,1,0:T(4,128)(2,1)}), bf16[128,4,384]{2,1,0:T(4,128)(2,1)S(1)}, u32[]{:S(2)}, u32[]{:S(2)}) %all-to-all-start.1) | async-done | bytes 393248 | tf_op jit(solution)/shard_map/all_to_all | solution.py:506
  79.6 1.0 copy-done.3
  80.6 1.0 copy-done.5
  81.6 8.7 %shard_map.103 = (bf16[4,8,24,384]{3,2,1,0:T(8,128)(2,1)S(1)}, bf16[4,8,24,384]{3,2,1,0:T(8,128)(2,1)}, bf16[512,384]{1,0:T(8,128)(2,1)S(1)}, bf16[384,512]{1,0:T(8,128)(2,1)S(1)}, bf16[512,768]{1,0:T(8,128)(2,1)S(1)}) custom-call(bf16[512,384]{1,0:T(8,128)(2,1)S(1)} %bitcast.29, bf16[128,4,384]{2,1,0:T(4,128)(2,1)S(1)} %copy-done.3, ...), custom_call_target="tpu_custom_call" | custom-call | flops 4000000000 | bytes 6193152 | tf_op jit(solution)/shard_map/pallas_call | solution.py:91
  90.6 1.2 add_convert_fusion.1.refs_0_
  91.8 0.9 collective-permute-start.1
  92.7 1.6 %collective-permute-start.2 = (bf16[8,24,384]{2,1,0:T(8,128)(2,1)S(1)}, bf16[8,24,384]{2,1,0:T(8,128)(2,1)S(1)}, u32[]{:S(2)}, u32[]{:S(2)}) collective-permute-start(bf16[8,24,384]{2,1,0:T(8,128)(2,1)S(1)} %get-tuple-element.35), channel_id=1, source_target_pairs={{0,64},{1,65},{2,66},{3,67},{4,68},{5,69},{6,70},{7,71},{8,72},{9,... | collective-permute-start | bytes 442376 | tf_op jit(solution)/shard_map/ppermute | solution.py:420
  94.3 1.1 collective-permute-start.3
  95.5 1.2 add_convert_fusion.refs_0_
  96.8 1.0 collective-permute-start.5
  97.7 2.0 %collective-permute-start.6 = (bf16[8,24,384]{2,1,0:T(8,128)(2,1)S(1)}, bf16[8,24,384]{2,1,0:T(8,128)(2,1)S(1)}, u32[]{:S(2)}, u32[]{:S(2)}) collective-permute-start(bf16[8,24,384]{2,1,0:T(8,128)(2,1)S(1)} %get-tuple-element.32), channel_id=1, source_target_pairs={{0,64},{1,65},{2,66},{3,67},{4,68},{5,69},{6,70},{7,71},{8,72},{9,... | collective-permute-start | bytes 442376 | tf_op jit(solution)/shard_map/ppermute | solution.py:420
  99.8 3.3 %collective-permute-done.1.refs_1_ = bf16[8,24,384]{2,1,0:T(8,128)(2,1)S(1)} collective-permute-done((bf16[8,24,384]{2,1,0:T(8,128)(2,1)S(1)}, bf16[8,24,384]{2,1,0:T(8,128)(2,1)S(1)}, u32[]{:S(2)}, u32[]{:S(2)}) %collective-permute-start.1) | collective-permute-done | bytes 147488 | tf_op jit(solution)/shard_map/ppermute | solution.py:420
  103.0 0.9 collective-permute-done.3.refs_3_
  104.0 4.6 %collective-permute-done.5.refs_1_ = bf16[8,24,384]{2,1,0:T(8,128)(2,1)S(1)} collective-permute-done((bf16[8,24,384]{2,1,0:T(8,128)(2,1)S(1)}, bf16[8,24,384]{2,1,0:T(8,128)(2,1)S(1)}, u32[]{:S(2)}, u32[]{:S(2)}) %collective-permute-start.5) | collective-permute-done | bytes 147488 | tf_op jit(solution)/shard_map/ppermute | solution.py:420
  109.5 14.4 %all_to_all.16 = bf16[16,24,384]{2,1,0:T(8,128)(2,1)S(1)} all-to-all(bf16[16,24,384]{2,1,0:T(8,128)(2,1)S(1)} %bitcast.24), channel_id=1, replica_groups={{0,2,4,6,8,10,12,14,16,18,20,22,24,26,28,30},{1,3,5,7,9,11,13,15,17,19,..., dimensions={0} | all-to-all | bytes 589824 | tf_op jit(solution)/shard_map/all_to_all | solution.py:489
  123.9 1.5 %collective-permute-start.8 = (bf16[24,384]{1,0:T(8,128)(2,1)S(1)}, bf16[24,384]{1,0:T(8,128)(2,1)S(1)}, u32[]{:S(2)}, u32[]{:S(2)}) collective-permute-start(bf16[24,384]{1,0:T(8,128)(2,1)S(1)} %reduce_sum.12), channel_id=1, source_target_pairs={{0,128},{128,0},{1,129},{129,1},{2,130},{130,2},{3,131},{131,3},{4... | collective-permute-start | bytes 55304 | tf_op jit(solution)/shard_map/ppermute | solution.py:493
  125.4 1.8 %shard_map.104 = bf16[512,384]{1,0:T(8,128)(2,1)} custom-call(bf16[512,384]{1,0:T(8,128)(2,1)S(1)} %bitcast.27, bf16[384,1152]{1,0:T(8,128)(2,1)S(1)} %copy-done, bf16[384,512]{1,0:T(8,128)(2,1)S(1)} %get-tuple-element.21.dqt_ref, bf16[512,768]{1,0:T(8,128)(2,1)S(1)} %get-tuple-element.22.dkv_ref, bf16[512,384]{1,0:T(8,128)(2,1)S(1)} %get-tuple-element.23.sg_ref), custom_call_target="tpu_custom_call" | custom-call | flops 500000000 | bytes 2850816 | tf_op jit(solution)/shard_map/pallas_call | solution.py:91
  (33 shorter events, 3.9 us)
Async XLA Ops:
  6.9 40.2 %copy-start.4 = (bf16[384,1152]{1,0:T(8,128)(2,1)S(1)}, bf16[384,1152]{1,0:T(8,128)(2,1)}, u32[]{:S(2)}) copy-start(bf16[384,1152]{1,0:T(8,128)(2,1)} %w_ref.2) | copy-start | bytes 2654212
  6.9 40.2 %copy-start.6 = (bf16[384,384]{1,0:T(8,128)(2,1)S(1)}, bf16[384,384]{1,0:T(8,128)(2,1)}, u32[]{:S(2)}) copy-start(bf16[384,384]{1,0:T(8,128)(2,1)} %wo_ref.2) | copy-start | bytes 884740
  52.6 1.0 copy-start.8
  53.7 25.2 %all-to-all-start.1 = ((bf16[128,4,384]{2,1,0:T(4,128)(2,1)}), bf16[128,4,384]{2,1,0:T(4,128)(2,1)S(1)}, u32[]{:S(2)}, u32[]{:S(2)}) async-start(bf16[128,4,384]{2,1,0:T(4,128)(2,1)} %get-tuple-element.19), calls=%async_computation.1 | async-start | bytes 786432 | tf_op jit(solution)/shard_map/all_to_all | solution.py:506
  60.9 1.3 copy-start.9
  62.2 17.5 %copy-start.1 = (bf16[1,1,512,384]{3,2,1,0:T(8,128)(2,1)S(1)}, bf16[1,1,512,384]{3,2,1,0:T(8,128)(2,1)}, u32[]{:S(2)}) copy-start(bf16[1,1,512,384]{3,2,1,0:T(8,128)(2,1)} %param.6) | copy-start | bytes 1179652
  62.2 17.5 %copy-start.7 = (bf16[384,384]{1,0:T(8,128)(2,1)S(1)}, bf16[384,384]{1,0:T(8,128)(2,1)}, u32[]{:S(2)}) copy-start(bf16[384,384]{1,0:T(8,128)(2,1)} %wo_ref.3) | copy-start | bytes 884740
  64.9 25.7 %collective-permute-start = (bf16[4,8,24,384]{3,2,1,0:T(8,128)(2,1)}, bf16[4,8,24,384]{3,2,1,0:T(8,128)(2,1)}, u32[]{:S(2)}, u32[]{:S(2)}) collective-permute-start(bf16[4,8,24,384]{3,2,1,0:T(8,128)(2,1)} %get-tuple-element.28), channel_id=1, source_target_pairs={{0,1},{1,0},{2,3},{3,2},{4,5},{5,4},{6,7},{7,6},{8,9},{9,8},{10,11... | collective-permute-start | bytes 1769480 | tf_op jit(solution)/shard_map/ppermute | solution.py:420
  78.9 0.7 copy-start.2
  79.6 1.0 copy-start.3
  80.6 1.0 copy-start.5
  90.3 5.2 %collective-permute-start.4 = (bf16[4,8,24,384]{3,2,1,0:T(8,128)(2,1)}, bf16[4,8,24,384]{3,2,1,0:T(8,128)(2,1)}, u32[]{:S(2)}, u32[]{:S(2)}) collective-permute-start(bf16[4,8,24,384]{3,2,1,0:T(8,128)(2,1)} %get-tuple-element.30), channel_id=1, source_target_pairs={{0,1},{1,0},{2,3},{3,2},{4,5},{5,4},{6,7},{7,6},{8,9},{9,8},{10,11... | collective-permute-start | bytes 1769480 | tf_op jit(solution)/shard_map/ppermute | solution.py:420
  91.8 11.2 %collective-permute-start.1 = (bf16[8,24,384]{2,1,0:T(8,128)(2,1)S(1)}, bf16[8,24,384]{2,1,0:T(8,128)(2,1)S(1)}, u32[]{:S(2)}, u32[]{:S(2)}) collective-permute-start(bf16[8,24,384]{2,1,0:T(8,128)(2,1)S(1)} %get-tuple-element.36), channel_id=1, source_target_pairs={{0,32},{1,33},{2,34},{3,35},{4,36},{5,37},{6,38},{7,39},{8,40},{9,... | collective-permute-start | bytes 442376 | tf_op jit(solution)/shard_map/ppermute | solution.py:420
  92.7 10.3 %collective-permute-start.2 = (bf16[8,24,384]{2,1,0:T(8,128)(2,1)S(1)}, bf16[8,24,384]{2,1,0:T(8,128)(2,1)S(1)}, u32[]{:S(2)}, u32[]{:S(2)}) collective-permute-start(bf16[8,24,384]{2,1,0:T(8,128)(2,1)S(1)} %get-tuple-element.35), channel_id=1, source_target_pairs={{0,64},{1,65},{2,66},{3,67},{4,68},{5,69},{6,70},{7,71},{8,72},{9,... | collective-permute-start | bytes 442376 | tf_op jit(solution)/shard_map/ppermute | solution.py:420
  94.3 9.6 %collective-permute-start.3 = (bf16[8,24,384]{2,1,0:T(8,128)(2,1)S(1)}, bf16[8,24,384]{2,1,0:T(8,128)(2,1)S(1)}, u32[]{:S(2)}, u32[]{:S(2)}) collective-permute-start(bf16[8,24,384]{2,1,0:T(8,128)(2,1)S(1)} %get-tuple-element.34), channel_id=1, source_target_pairs={{0,96},{1,97},{2,98},{3,99},{4,100},{5,101},{6,102},{7,103},{8,104... | collective-permute-start | bytes 442376 | tf_op jit(solution)/shard_map/ppermute | solution.py:420
  96.8 11.9 %collective-permute-start.5 = (bf16[8,24,384]{2,1,0:T(8,128)(2,1)S(1)}, bf16[8,24,384]{2,1,0:T(8,128)(2,1)S(1)}, u32[]{:S(2)}, u32[]{:S(2)}) collective-permute-start(bf16[8,24,384]{2,1,0:T(8,128)(2,1)S(1)} %get-tuple-element.33), channel_id=1, source_target_pairs={{0,32},{1,33},{2,34},{3,35},{4,36},{5,37},{6,38},{7,39},{8,40},{9,... | collective-permute-start | bytes 442376 | tf_op jit(solution)/shard_map/ppermute | solution.py:420
  97.7 11.0 %collective-permute-start.6 = (bf16[8,24,384]{2,1,0:T(8,128)(2,1)S(1)}, bf16[8,24,384]{2,1,0:T(8,128)(2,1)S(1)}, u32[]{:S(2)}, u32[]{:S(2)}) collective-permute-start(bf16[8,24,384]{2,1,0:T(8,128)(2,1)S(1)} %get-tuple-element.32), channel_id=1, source_target_pairs={{0,64},{1,65},{2,66},{3,67},{4,68},{5,69},{6,70},{7,71},{8,72},{9,... | collective-permute-start | bytes 442376 | tf_op jit(solution)/shard_map/ppermute | solution.py:420
  103.0 6.3 %collective-permute-start.7 = (bf16[8,24,384]{2,1,0:T(8,128)(2,1)S(1)}, bf16[8,24,384]{2,1,0:T(8,128)(2,1)S(1)}, u32[]{:S(2)}, u32[]{:S(2)}) collective-permute-start(bf16[8,24,384]{2,1,0:T(8,128)(2,1)S(1)} %get-tuple-element.31), channel_id=1, source_target_pairs={{0,96},{1,97},{2,98},{3,99},{4,100},{5,101},{6,102},{7,103},{8,104... | collective-permute-start | bytes 442376 | tf_op jit(solution)/shard_map/ppermute | solution.py:420
  104.0 21.4 %copy-start = (bf16[384,1152]{1,0:T(8,128)(2,1)S(1)}, bf16[384,1152]{1,0:T(8,128)(2,1)}, u32[]{:S(2)}) copy-start(bf16[384,1152]{1,0:T(8,128)(2,1)} %w_ref.3) | copy-start | bytes 2654212
  123.9 3.8 %collective-permute-start.8 = (bf16[24,384]{1,0:T(8,128)(2,1)S(1)}, bf16[24,384]{1,0:T(8,128)(2,1)S(1)}, u32[]{:S(2)}, u32[]{:S(2)}) collective-permute-start(bf16[24,384]{1,0:T(8,128)(2,1)S(1)} %reduce_sum.12), channel_id=1, source_target_pairs={{0,128},{128,0},{1,129},{129,1},{2,130},{130,2},{3,131},{131,3},{4... | collective-permute-start | bytes 55304 | tf_op jit(solution)/shard_map/ppermute | solution.py:493

commit v5 on v4

--- a/solution.py
+++ b/solution.py
@@ -452,7 +452,7 @@
     here, size = coordinate("x"), part.shape[0]
     return (part,) + tuple(
         shift(lax.dynamic_index_in_dim(part, (here + k) % size, 0, keepdims=False), "x", k)
-        for k in range(1, size)
+        for k in sorted(range(1, size), key=lambda k: -min(k, size - k))
     )
 
 
@@ -490,8 +490,26 @@
         flat, "seq", split_axis=0, concat_axis=0, tiled=True, axis_index_groups=groups_of("yh", "z")
     )
     mine = jnp.sum(got.astype(F32), 0).astype(B16)
-    other = lax.ppermute(mine, "dp", [(0, 1), (1, 0)])
-    return mine.astype(F32) + other.astype(F32)
+    return mine, lax.ppermute(mine, "dp", [(0, 1), (1, 0)])
+
+
+def share_kernel(mine_ref, other_ref, *out_refs):
+    total = mine_ref[...].astype(F32) + other_ref[...].astype(F32)
+    start = 0
+    for ref in out_refs:
+        ref[...] = total[start : start + ref.shape[0]]
+        start += ref.shape[0]
+
+
+def shares_of(mine, other, counts):
+    return pl.pallas_call(
+        share_kernel,
+        out_shape=tuple(jax.ShapeDtypeStruct((n, mine.shape[1]), F32) for n in counts),
+        in_specs=[VM] * 2,
+        out_specs=(VM,) * len(counts),
+        compiler_params=pltpu.CompilerParams(vmem_limit_bytes=48 << 20),
+        name="shares",
+    )(mine, other)
 
 
 def on_device(tokens, cotangent, wqkv_spatial, wo_spatial, wqkv_temporal, wo_temporal):
@@ -517,9 +535,9 @@
     token_grad = token_gradient(tok, wqkv_spatial, dqt, dkv, stream_grad)
     half_t = sum_early(half_t)
     joined = join(half_t, half_s)
-    own = last_stages(joined)
+    mine, other = last_stages(joined)
     a, b = 3 * width // seq_size(), width // seq_size()
-    shares = (own[:a].T, own[a : a + b].T, own[a + b : 2 * a + b].T, own[2 * a + b :].T)
+    shares = [share.T for share in shares_of(mine, other, (a, b, a, b))]
     return (token_grad.reshape(tokens.shape), *shares)
 
 

time: 131 us -> 130 us (level)
  waiting for transfers between devices: 23.8 us -> 21.8 us
  starting transfers between devices: 15.8 us -> 17.4 us
    ppermute x8, waiting for transfers between devices: 9.46 us -> 7.34 us  [shift(): return lax.ppermute(array, 'seq', pairs)]
    ppermute x8, starting transfers between devices: 7.02 us -> 8.78 us  [shift(): return lax.ppermute(array, 'seq', pairs)]
where the time goes in v5:
time: 130 us; the launch traced here: 129 us
  blocking collectives  55.4 us (43%)
  Pallas kernels  25.8 us (20%)
  waiting for transfers between devices  21.8 us (17%)
  starting transfers between devices  17.4 us (13%)
  local copies, waits for them, and re-layouts  5.18 us (4%)
  other arithmetic  2.47 us (2%)
    all_to_all x1, blocking collectives, trade(): return lax.all_to_all(array, 'seq', split_axis=0, concat_axis=0, tiled=True)  40.2 us
    pallas_call x7, Pallas kernels, call(): pl.pallas_call(kernel, out_shape=tuple((jax.ShapeDtypeStruct(shape, B16)...  25.1 us
    all_to_all x1, blocking collectives, last_stages(): lax.all_to_all(flat, 'seq', split_axis=0, concat_axis=0, tiled=True, axis...  15.2 us
    all_to_all x1, waiting for transfers between devices, trade(): return lax.all_to_all(array, 'seq', split_axis=0, concat_axis=0, tiled=True)  13.9 us
    ppermute x8, starting transfers between devices, shift(): return lax.ppermute(array, 'seq', pairs)  8.78 us
    ppermute x8, waiting for transfers between devices, shift(): return lax.ppermute(array, 'seq', pairs)  7.34 us
    all_to_all x1, starting transfers between devices, trade(): return lax.all_to_all(array, 'seq', split_axis=0, concat_axis=0, tiled=True)  7.22 us
    unnamed x20, local copies, waits for them, and re-layouts  5.07 us
  transfers between devices with their start and end apart: 10, of which 6 were waited for; matrix products, arithmetic and copies ran while one was open for 2% of the time, Pallas kernels for 10%

profile of v5, /device:TPU:8, one launch (start us, length us, event | category | flops | bytes accessed | tf_op | source)
XLA Modules:
  0.0 128.9 jit_solution(2924266870404534216)
XLA Ops:
  0.6 6.3 %shard_map.101 = (bf16[128,2,4,384]{3,2,1,0:T(4,128)(2,1)}, bf16[9,512,512]{2,1,0:T(8,128)(2,1)}) custom-call(bf16[512,384]{1,0:T(8,128)(2,1)} %bitcast.21, bf16[512,384]{1,0:T(8,128)(2,1)} %bitcast.24, bf16[384,1152]{1,0:T(8,128)(2,1)} %w_ref.3, bf16[384,384]{1,0:T(8,128)(2,1)} %wo_ref.3), custom_call_target="tpu_custom_call" | custom-call | flops 2000000000 | bytes 1966080 | tf_op jit(solution)/shard_map/pallas_call | solution.py:91
  6.9 40.2 %all_to_all.15.slab_ref = bf16[128,2,4,384]{3,2,1,0:T(4,128)(2,1)S(1)} all-to-all(bf16[128,2,4,384]{3,2,1,0:T(4,128)(2,1)} %get-tuple-element.22), channel_id=1, replica_groups=mesh['dp'=2,'seq'=128] {'seq'}, dimensions={0} | all-to-all | bytes 1572864 | tf_op jit(solution)/shard_map/all_to_all | solution.py:524
  47.1 5.5 %shard_map.102 = (bf16[128,4,384]{2,1,0:T(4,128)(2,1)}, bf16[512,384]{1,0:T(8,128)(2,1)S(1)}, bf16[384,384]{1,0:T(8,128)(2,1)S(1)}, bf16[1152,512]{1,0:T(8,128)(2,1)S(1)}) custom-call(bf16[128,2,4,384]{3,2,1,0:T(4,128)(2,1)S(1)} %all_to_all.15.slab_ref, bf16[384,1152]{1,0:T(8,128)(2,1)S(1)} %copy-done.4, bf16[384,384]{1,0:T(8,128)(2,1)S(1)} %copy-done.6), custom_call_target="tpu_custom_call" | custom-call | flops 3000000000 | bytes 1966080 | tf_op jit(solution)/shard_map/pallas_call | solution.py:91
  52.6 1.0 copy-done.8
  53.7 7.2 %all-to-all-start.1 = ((bf16[128,4,384]{2,1,0:T(4,128)(2,1)}), bf16[128,4,384]{2,1,0:T(4,128)(2,1)S(1)}, u32[]{:S(2)}, u32[]{:S(2)}) async-start(bf16[128,4,384]{2,1,0:T(4,128)(2,1)} %get-tuple-element.23), calls=%async_computation.1 | async-start | bytes 786432 | tf_op jit(solution)/shard_map/all_to_all | solution.py:524
  60.9 1.3 copy-done.9
  62.2 2.7 %shard_map.105 = (bf16[4,8,24,384]{3,2,1,0:T(8,128)(2,1)S(1)}, bf16[4,8,24,384]{3,2,1,0:T(8,128)(2,1)}) custom-call(bf16[512,384]{1,0:T(8,128)(2,1)S(1)} %get-tuple-element.28.normed_ref, bf16[384,384]{1,0:T(8,128)(2,1)S(1)} %get-tuple-element.29.go_ref, bf16[1152,512]{1,0:T(8,128)(2,1)S(1)} %copy-done.9), custom_call_target="tpu_custom_call" | custom-call | flops 1500000000 | bytes 1867776 | tf_op jit(solution)/shard_map/pallas_call | solution.py:91
  65.0 13.9 %all-to-all-done.1.br_ref = bf16[128,4,384]{2,1,0:T(4,128)(2,1)S(1)} async-done(((bf16[128,4,384]{2,1,0:T(4,128)(2,1)}), bf16[128,4,384]{2,1,0:T(4,128)(2,1)S(1)}, u32[]{:S(2)}, u32[]{:S(2)}) %all-to-all-start.1) | async-done | bytes 393248 | tf_op jit(solution)/shard_map/all_to_all | solution.py:524
  79.6 1.0 copy-done.3
  80.6 1.0 copy-done.5
  81.6 8.6 %shard_map.103 = (bf16[4,8,24,384]{3,2,1,0:T(8,128)(2,1)S(1)}, bf16[4,8,24,384]{3,2,1,0:T(8,128)(2,1)}, bf16[512,384]{1,0:T(8,128)(2,1)S(1)}, bf16[384,512]{1,0:T(8,128)(2,1)S(1)}, bf16[512,768]{1,0:T(8,128)(2,1)S(1)}) custom-call(bf16[512,384]{1,0:T(8,128)(2,1)S(1)} %bitcast.25, bf16[128,4,384]{2,1,0:T(4,128)(2,1)S(1)} %copy-done.3, ...), custom_call_target="tpu_custom_call" | custom-call | flops 4000000000 | bytes 6193152 | tf_op jit(solution)/shard_map/pallas_call | solution.py:91
  90.5 1.2 add_convert_fusion.1.refs_0_
  91.8 0.8 collective-permute-start.1
  92.7 1.1 collective-permute-start.2
  93.7 2.2 %collective-permute-start.3 = (bf16[8,24,384]{2,1,0:T(8,128)(2,1)S(1)}, bf16[8,24,384]{2,1,0:T(8,128)(2,1)S(1)}, u32[]{:S(2)}, u32[]{:S(2)}) collective-permute-start(bf16[8,24,384]{2,1,0:T(8,128)(2,1)S(1)} %get-tuple-element.42), channel_id=1, source_target_pairs={{0,96},{1,97},{2,98},{3,99},{4,100},{5,101},{6,102},{7,103},{8,104... | collective-permute-start | bytes 442376 | tf_op jit(solution)/shard_map/ppermute | solution.py:420
  95.9 1.2 add_convert_fusion.refs_0_
  97.2 1.7 %collective-permute-start.5 = (bf16[8,24,384]{2,1,0:T(8,128)(2,1)S(1)}, bf16[8,24,384]{2,1,0:T(8,128)(2,1)S(1)}, u32[]{:S(2)}, u32[]{:S(2)}) collective-permute-start(bf16[8,24,384]{2,1,0:T(8,128)(2,1)S(1)} %get-tuple-element.41), channel_id=1, source_target_pairs={{0,64},{1,65},{2,66},{3,67},{4,68},{5,69},{6,70},{7,71},{8,72},{9,... | collective-permute-start | bytes 442376 | tf_op jit(solution)/shard_map/ppermute | solution.py:420
  100.2 1.9 %collective-permute-start.7 = (bf16[8,24,384]{2,1,0:T(8,128)(2,1)S(1)}, bf16[8,24,384]{2,1,0:T(8,128)(2,1)S(1)}, u32[]{:S(2)}, u32[]{:S(2)}) collective-permute-start(bf16[8,24,384]{2,1,0:T(8,128)(2,1)S(1)} %get-tuple-element.39), channel_id=1, source_target_pairs={{0,96},{1,97},{2,98},{3,99},{4,100},{5,101},{6,102},{7,103},{8,104... | collective-permute-start | bytes 442376 | tf_op jit(solution)/shard_map/ppermute | solution.py:420
  102.1 1.3 %collective-permute-done.2.refs_2_ = bf16[8,24,384]{2,1,0:T(8,128)(2,1)S(1)} collective-permute-done((bf16[8,24,384]{2,1,0:T(8,128)(2,1)S(1)}, bf16[8,24,384]{2,1,0:T(8,128)(2,1)S(1)}, u32[]{:S(2)}, u32[]{:S(2)}) %collective-permute-start.2) | collective-permute-done | bytes 147488 | tf_op jit(solution)/shard_map/ppermute | solution.py:420
  103.5 3.0 %collective-permute-done.5.refs_1_ = bf16[8,24,384]{2,1,0:T(8,128)(2,1)S(1)} collective-permute-done((bf16[8,24,384]{2,1,0:T(8,128)(2,1)S(1)}, bf16[8,24,384]{2,1,0:T(8,128)(2,1)S(1)}, u32[]{:S(2)}, u32[]{:S(2)}) %collective-permute-start.5) | collective-permute-done | bytes 147488 | tf_op jit(solution)/shard_map/ppermute | solution.py:420
  106.5 2.4 %collective-permute-done.6.refs_2_ = bf16[8,24,384]{2,1,0:T(8,128)(2,1)S(1)} collective-permute-done((bf16[8,24,384]{2,1,0:T(8,128)(2,1)S(1)}, bf16[8,24,384]{2,1,0:T(8,128)(2,1)S(1)}, u32[]{:S(2)}, u32[]{:S(2)}) %collective-permute-start.6) | collective-permute-done | bytes 147488 | tf_op jit(solution)/shard_map/ppermute | solution.py:420
  109.1 15.2 %all_to_all.16 = bf16[16,24,384]{2,1,0:T(8,128)(2,1)S(1)} all-to-all(bf16[16,24,384]{2,1,0:T(8,128)(2,1)S(1)} %bitcast.20), channel_id=1, replica_groups={{0,2,4,6,8,10,12,14,16,18,20,22,24,26,28,30},{1,3,5,7,9,11,13,15,17,19,..., dimensions={0} | all-to-all | bytes 589824 | tf_op jit(solution)/shard_map/all_to_all | solution.py:489
  124.4 1.4 %collective-permute-start.8 = (bf16[24,384]{1,0:T(8,128)(2,1)S(1)}, bf16[24,384]{1,0:T(8,128)(2,1)S(1)}, u32[]{:S(2)}, u32[]{:S(2)}) collective-permute-start(bf16[24,384]{1,0:T(8,128)(2,1)S(1)} %reduce_sum.12.mine_ref), channel_id=1, source_target_pairs={{0,128},{128,0},{1,129},{129,1},{2,130},{130,2},{3,131},{131,3},{4... | collective-permute-start | bytes 55304 | tf_op jit(solution)/shard_map/ppermute | solution.py:493
  125.8 1.8 %shard_map.104 = bf16[512,384]{1,0:T(8,128)(2,1)} custom-call(bf16[512,384]{1,0:T(8,128)(2,1)S(1)} %bitcast.23, bf16[384,1152]{1,0:T(8,128)(2,1)S(1)} %copy-done, bf16[384,512]{1,0:T(8,128)(2,1)S(1)} %get-tuple-element.25.dqt_ref, bf16[512,768]{1,0:T(8,128)(2,1)S(1)} %get-tuple-element.26.dkv_ref, bf16[512,384]{1,0:T(8,128)(2,1)S(1)} %get-tuple-element.27.sg_ref), custom_call_target="tpu_custom_call" | custom-call | flops 500000000 | bytes 2850816 | tf_op jit(solution)/shard_map/pallas_call | solution.py:91
  (31 shorter events, 4.1 us)
Async XLA Ops:
  6.9 40.2 %copy-start.4 = (bf16[384,1152]{1,0:T(8,128)(2,1)S(1)}, bf16[384,1152]{1,0:T(8,128)(2,1)}, u32[]{:S(2)}) copy-start(bf16[384,1152]{1,0:T(8,128)(2,1)} %w_ref.2) | copy-start | bytes 2654212
  6.9 40.2 %copy-start.6 = (bf16[384,384]{1,0:T(8,128)(2,1)S(1)}, bf16[384,384]{1,0:T(8,128)(2,1)}, u32[]{:S(2)}) copy-start(bf16[384,384]{1,0:T(8,128)(2,1)} %wo_ref.2) | copy-start | bytes 884740
  52.6 1.0 copy-start.8
  53.7 25.2 %all-to-all-start.1 = ((bf16[128,4,384]{2,1,0:T(4,128)(2,1)}), bf16[128,4,384]{2,1,0:T(4,128)(2,1)S(1)}, u32[]{:S(2)}, u32[]{:S(2)}) async-start(bf16[128,4,384]{2,1,0:T(4,128)(2,1)} %get-tuple-element.23), calls=%async_computation.1 | async-start | bytes 786432 | tf_op jit(solution)/shard_map/all_to_all | solution.py:524
  60.9 1.3 copy-start.9
  62.2 17.4 %copy-start.1 = (bf16[1,1,512,384]{3,2,1,0:T(8,128)(2,1)S(1)}, bf16[1,1,512,384]{3,2,1,0:T(8,128)(2,1)}, u32[]{:S(2)}) copy-start(bf16[1,1,512,384]{3,2,1,0:T(8,128)(2,1)} %param.6) | copy-start | bytes 1179652
  62.2 17.5 %copy-start.7 = (bf16[384,384]{1,0:T(8,128)(2,1)S(1)}, bf16[384,384]{1,0:T(8,128)(2,1)}, u32[]{:S(2)}) copy-start(bf16[384,384]{1,0:T(8,128)(2,1)} %wo_ref.3) | copy-start | bytes 884740
  64.9 25.7 %collective-permute-start = (bf16[4,8,24,384]{3,2,1,0:T(8,128)(2,1)}, bf16[4,8,24,384]{3,2,1,0:T(8,128)(2,1)}, u32[]{:S(2)}, u32[]{:S(2)}) collective-permute-start(bf16[4,8,24,384]{3,2,1,0:T(8,128)(2,1)} %get-tuple-element.32), channel_id=1, source_target_pairs={{0,1},{1,0},{2,3},{3,2},{4,5},{5,4},{6,7},{7,6},{8,9},{9,8},{10,11... | collective-permute-start | bytes 1769480 | tf_op jit(solution)/shard_map/ppermute | solution.py:420
  78.9 0.7 copy-start.2
  79.6 1.0 copy-start.3
  80.6 1.0 copy-start.5
  90.3 5.6 %collective-permute-start.4 = (bf16[4,8,24,384]{3,2,1,0:T(8,128)(2,1)}, bf16[4,8,24,384]{3,2,1,0:T(8,128)(2,1)}, u32[]{:S(2)}, u32[]{:S(2)}) collective-permute-start(bf16[4,8,24,384]{3,2,1,0:T(8,128)(2,1)} %get-tuple-element.34), channel_id=1, source_target_pairs={{0,1},{1,0},{2,3},{3,2},{4,5},{5,4},{6,7},{7,6},{8,9},{9,8},{10,11... | collective-permute-start | bytes 1769480 | tf_op jit(solution)/shard_map/ppermute | solution.py:420
  91.8 8.4 %collective-permute-start.1 = (bf16[8,24,384]{2,1,0:T(8,128)(2,1)S(1)}, bf16[8,24,384]{2,1,0:T(8,128)(2,1)S(1)}, u32[]{:S(2)}, u32[]{:S(2)}) collective-permute-start(bf16[8,24,384]{2,1,0:T(8,128)(2,1)S(1)} %get-tuple-element.44), channel_id=1, source_target_pairs={{0,64},{1,65},{2,66},{3,67},{4,68},{5,69},{6,70},{7,71},{8,72},{9,... | collective-permute-start | bytes 442376 | tf_op jit(solution)/shard_map/ppermute | solution.py:420
  92.7 10.7 %collective-permute-start.2 = (bf16[8,24,384]{2,1,0:T(8,128)(2,1)S(1)}, bf16[8,24,384]{2,1,0:T(8,128)(2,1)S(1)}, u32[]{:S(2)}, u32[]{:S(2)}) collective-permute-start(bf16[8,24,384]{2,1,0:T(8,128)(2,1)S(1)} %get-tuple-element.43), channel_id=1, source_target_pairs={{0,32},{1,33},{2,34},{3,35},{4,36},{5,37},{6,38},{7,39},{8,40},{9,... | collective-permute-start | bytes 442376 | tf_op jit(solution)/shard_map/ppermute | solution.py:420
  93.7 9.7 %collective-permute-start.3 = (bf16[8,24,384]{2,1,0:T(8,128)(2,1)S(1)}, bf16[8,24,384]{2,1,0:T(8,128)(2,1)S(1)}, u32[]{:S(2)}, u32[]{:S(2)}) collective-permute-start(bf16[8,24,384]{2,1,0:T(8,128)(2,1)S(1)} %get-tuple-element.42), channel_id=1, source_target_pairs={{0,96},{1,97},{2,98},{3,99},{4,100},{5,101},{6,102},{7,103},{8,104... | collective-permute-start | bytes 442376 | tf_op jit(solution)/shard_map/ppermute | solution.py:420
  97.2 9.4 %collective-permute-start.5 = (bf16[8,24,384]{2,1,0:T(8,128)(2,1)S(1)}, bf16[8,24,384]{2,1,0:T(8,128)(2,1)S(1)}, u32[]{:S(2)}, u32[]{:S(2)}) collective-permute-start(bf16[8,24,384]{2,1,0:T(8,128)(2,1)S(1)} %get-tuple-element.41), channel_id=1, source_target_pairs={{0,64},{1,65},{2,66},{3,67},{4,68},{5,69},{6,70},{7,71},{8,72},{9,... | collective-permute-start | bytes 442376 | tf_op jit(solution)/shard_map/ppermute | solution.py:420
  98.8 10.1 %collective-permute-start.6 = (bf16[8,24,384]{2,1,0:T(8,128)(2,1)S(1)}, bf16[8,24,384]{2,1,0:T(8,128)(2,1)S(1)}, u32[]{:S(2)}, u32[]{:S(2)}) collective-permute-start(bf16[8,24,384]{2,1,0:T(8,128)(2,1)S(1)} %get-tuple-element.40), channel_id=1, source_target_pairs={{0,32},{1,33},{2,34},{3,35},{4,36},{5,37},{6,38},{7,39},{8,40},{9,... | collective-permute-start | bytes 442376 | tf_op jit(solution)/shard_map/ppermute | solution.py:420
  100.2 8.8 %collective-permute-start.7 = (bf16[8,24,384]{2,1,0:T(8,128)(2,1)S(1)}, bf16[8,24,384]{2,1,0:T(8,128)(2,1)S(1)}, u32[]{:S(2)}, u32[]{:S(2)}) collective-permute-start(bf16[8,24,384]{2,1,0:T(8,128)(2,1)S(1)} %get-tuple-element.39), channel_id=1, source_target_pairs={{0,96},{1,97},{2,98},{3,99},{4,100},{5,101},{6,102},{7,103},{8,104... | collective-permute-start | bytes 442376 | tf_op jit(solution)/shard_map/ppermute | solution.py:420
  103.5 22.3 %copy-start = (bf16[384,1152]{1,0:T(8,128)(2,1)S(1)}, bf16[384,1152]{1,0:T(8,128)(2,1)}, u32[]{:S(2)}) copy-start(bf16[384,1152]{1,0:T(8,128)(2,1)} %w_ref.3) | copy-start | bytes 2654212
  124.4 3.8 %collective-permute-start.8 = (bf16[24,384]{1,0:T(8,128)(2,1)S(1)}, bf16[24,384]{1,0:T(8,128)(2,1)S(1)}, u32[]{:S(2)}, u32[]{:S(2)}) collective-permute-start(bf16[24,384]{1,0:T(8,128)(2,1)S(1)} %reduce_sum.12.mine_ref), channel_id=1, source_target_pairs={{0,128},{128,0},{1,129},{129,1},{2,130},{130,2},{3,131},{131,3},{4... | collective-permute-start | bytes 55304 | tf_op jit(solution)/shard_map/ppermute | solution.py:493
